TPU v7x, 512 devices: a whole 4x4x16 slice. The times are simulated.
512 devices in a mesh: row: 32 (over z_lo, y), col: 16 (over x, z_hi, core).
Axes of the slice: x: 4, y: 4, z: 16 (z_hi: 2, z_lo: 8; z = z_hi * 8 + z_lo), core: 2. Of those that a mesh axis runs over, the one named last changes fastest.
Arguments:
- pair_slab: bfloat16 [64, 1024, 128], P('col', 'row'), may hold values from -6 to 6
- pair_full: bfloat16 [1024, 1024, 128], P('col', 'row'), may hold values from -6 to 6
- grad_out: bfloat16 [64, 1024, 128], P('row', 'col'), may hold values from -0.59765625 to 0.59765625
- w_a_lin: bfloat16 [128, 128], replicated, may hold values from -0.5 to 0.5
- w_a_gate: bfloat16 [128, 128], replicated, may hold values from -0.5 to 0.5
- w_b_lin: bfloat16 [128, 128], replicated, may hold values from -0.5 to 0.5
- w_b_gate: bfloat16 [128, 128], replicated, may hold values from -0.5 to 0.5
- mask_slab: int32 [64], replicated, may hold values 0 or 1
- mask_residue: int32 [1024], replicated, may hold values 0 or 1
Outputs:
- grad_slab: bfloat16 [64, 1024, 128], P('col', 'row')
- grad_pair: bfloat16 [1024, 1024, 128], P('col', 'row')
- grad_weights: float32 [4, 128, 128], replicated
All inputs are finite; a program needn't handle non-finite values.
Results may differ from a plain program's by a relative error of at most 0.0057.
Values may be sent and summed in bfloat16 or wider, within the bound.
A program may use at most 64 MiB of HBM per device.

v0:
```python
import jax
import jax.numpy as jnp
from jax import lax
from jax.sharding import PartitionSpec as P


def forward_gate(pair, w_linear, w_gate, mask):
    linear = jnp.einsum("rkd,dc->rkc", pair, w_linear, preferred_element_type=jnp.float32)
    gate = jnp.einsum("rkd,dc->rkc", pair, w_gate, preferred_element_type=jnp.float32)
    sigmoid = jax.nn.sigmoid(gate)
    value = (mask * sigmoid * linear).astype(jnp.bfloat16)
    return (linear, sigmoid, value)


def gate_back(grad, mask, linear, sigmoid):
    d_linear = (grad * mask * sigmoid).astype(jnp.bfloat16)
    d_gate = (grad * mask * linear * sigmoid * (1.0 - sigmoid)).astype(jnp.bfloat16)
    return (d_linear, d_gate)


def input_grads(pair, d_linear, d_gate, w_linear, w_gate):
    input_grad = jnp.einsum("rkc,dc->rkd", d_linear, w_linear, preferred_element_type=jnp.float32)
    input_grad = input_grad + jnp.einsum(
        "rkc,dc->rkd", d_gate, w_gate, preferred_element_type=jnp.float32
    )
    weight_linear = jnp.einsum("rkd,rkc->dc", pair, d_linear, preferred_element_type=jnp.float32)
    weight_gate = jnp.einsum("rkd,rkc->dc", pair, d_gate, preferred_element_type=jnp.float32)
    return (input_grad.astype(jnp.bfloat16), weight_linear, weight_gate)


def on_device(
    pair_slab, pair_full, grad_out, w_a_lin, w_a_gate, w_b_lin, w_b_gate, mask_slab, mask_residue
):
    own_rows = pair_slab.shape[0]
    own_keys = pair_slab.shape[1]
    own_cols = pair_full.shape[0]
    row_index = lax.axis_index("row")
    col_index = lax.axis_index("col")
    slab_flags = lax.dynamic_slice_in_dim(mask_slab, col_index * own_rows, own_rows).astype(
        jnp.float32
    )
    key_flags = lax.dynamic_slice_in_dim(mask_residue, row_index * own_keys, own_keys).astype(
        jnp.float32
    )
    col_flags = lax.dynamic_slice_in_dim(mask_residue, col_index * own_cols, own_cols).astype(
        jnp.float32
    )
    slab_mask = (slab_flags[:, None] * key_flags[None, :])[:, :, None]
    pair_mask = (col_flags[:, None] * key_flags[None, :])[:, :, None]
    slab_linear, slab_sigmoid, slab_value = forward_gate(pair_slab, w_a_lin, w_a_gate, slab_mask)
    slab_all = lax.all_gather(slab_value, "col", axis=0, tiled=True)
    grad_all = lax.all_gather(grad_out, "row", axis=0, tiled=True)
    pair_linear, pair_sigmoid, pair_value = forward_gate(pair_full, w_b_lin, w_b_gate, pair_mask)
    pair_grad = jnp.einsum("ijc,ikc->jkc", grad_all, slab_all, preferred_element_type=jnp.float32)
    pair_dlin, pair_dgate = gate_back(pair_grad, pair_mask, pair_linear, pair_sigmoid)
    grad_pair, pair_lin_w, pair_gate_w = input_grads(
        pair_full, pair_dlin, pair_dgate, w_b_lin, w_b_gate
    )
    partial_value = jnp.einsum(
        "ijc,jkc->ikc", grad_all, pair_value, preferred_element_type=jnp.float32
    )
    summed = lax.psum(partial_value, "col")
    slab_grad = lax.dynamic_slice_in_dim(summed, col_index * own_rows, own_rows, 0)
    slab_dlin, slab_dgate = gate_back(slab_grad, slab_mask, slab_linear, slab_sigmoid)
    grad_slab, slab_lin_w, slab_gate_w = input_grads(
        pair_slab, slab_dlin, slab_dgate, w_a_lin, w_a_gate
    )
    local_weights = jnp.stack([slab_lin_w, slab_gate_w, pair_lin_w, pair_gate_w])
    total_weights = lax.psum(local_weights, ("row", "col"))
    residues = own_keys * lax.axis_size("row")
    grad_weights = total_weights / residues
    return (grad_slab, grad_pair, grad_weights)


def solution(mesh):
    return jax.shard_map(
        on_device,
        mesh=mesh,
        in_specs=(
            P("col", "row", None),
            P("col", "row", None),
            P("row", "col", None),
            P(),
            P(),
            P(),
            P(),
            P(),
            P(),
        ),
        out_specs=(P("col", "row", None), P("col", "row", None), P()),
        check_vma=False,
    )
```

profile of v0, /device:TPU:1, one launch (start us, length us, event | category | flops | bytes accessed | tf_op | source)
XLA Modules:
  0.0 1022.2 jit_solution(12804683409125686854)
XLA Ops:
  7.2 0.7 all-gather.2.cloned.1.call-update
  8.0 0.7 dynamic-slice_convert_fusion
  8.7 0.8 dynamic-slice_convert_fusion.1
  9.5 0.9 fusion.6
  10.5 0.9 multiply_convert_fusion.3
  11.4 63.7 %all_gather.7 = bf16[64,32,128]{2,1,0:T(8,128)(2,1)S(1)} all-gather(bf16[4,32,128]{2,1,0:T(8,128)(2,1)S(1)} %get-tuple-element.17), channel_id=1, replica_groups=mesh['row'=32,'col'=16] {'col'}, dimensions={0}, use_global_device_ids=true | all-gather | bytes 557056 | tf_op jit(solution)/shard_map/all_gather | solution.py:51
  75.1 3.7 copy.49
  78.9 0.8 dynamic-slice_convert_fusion.2
  79.6 0.1 broadcast_multiply_fusion.1
  79.7 1.2 fusion.16
  80.9 137.6 %all-gather.2.cloned.1.call-done = bf16[64,64,128]{2,1,0:T(8,128)(2,1)} async-done(((bf16[2,64,128]{2,1,0:T(8,128)(2,1)}), bf16[64,64,128]{2,1,0:T(8,128)(2,1)}) %all-gather.2.cloned.1.call-update) | async-done | bytes 1048592 | tf_op jit(solution)/shard_map/all_gather | solution.py:52
  218.6 3.9 copy.47
  222.5 3.6 fusion.21
  226.2 3.9 copy.51
  230.1 3.2 multiply_convert_fusion
  233.3 3.7 copy.46
  236.9 3.8 fusion.20
  240.7 3.9 copy.48
  244.7 0.3 convolution_bitcast_fusion
  245.1 0.3 convolution_bitcast_fusion.1
  245.4 0.3 fusion.14
  245.8 1.1 fusion.3
  246.8 298.6 %all-reduce.3.cloned.1.call-done = f32[64,32,128]{2,1,0:T(8,128)} async-done(((f32[64,32,128]{2,1,0:T(8,128)}), f32[64,32,128]{2,1,0:T(8,128)}) %all-reduce.3.cloned.1.call-update) | async-done | bytes 1048592 | tf_op jit(solution)/shard_map/psum | solution.py:62
  545.4 0.9 multiply_convert_fusion.4
  546.3 0.2 convolution_bitcast_fusion.3
  546.5 0.1 fusion.10
  546.7 0.2 convolution_bitcast_fusion.2
  546.9 0.7 pad_maximum_fusion
  547.6 0.8 fusion.7
  548.4 465.5 %all-reduce.5.cloned.1.call-done = f32[4,128,128]{1,2,0:T(8,128)} async-done(((f32[4,128,128]{1,2,0:T(8,128)}), f32[4,128,128]{1,2,0:T(8,128)}) %all-reduce.5.cloned.1.call-update) | async-done | bytes 262160 | tf_op jit(solution)/shard_map/psum | solution.py:69
  1013.9 1.0 broadcast_multiply_fusion
  1014.9 0.8 copy.52
  (20 shorter events, 0.3 us)
Async XLA Ops:
  7.2 72.5 %copy-start = (bf16[64,32,128]{2,1,0:T(8,128)(2,1)S(1)}, bf16[64,32,128]{2,1,0:T(8,128)(2,1)}, u32[]{:S(2)}) copy-start(bf16[64,32,128]{2,1,0:T(8,128)(2,1)} %param.10) | copy-start | bytes 1572868
  7.2 72.5 %copy-start.3 = (bf16[128,128]{1,0:T(8,128)(2,1)S(1)}, bf16[128,128]{1,0:T(8,128)(2,1)}, u32[]{:S(2)}) copy-start(bf16[128,128]{1,0:T(8,128)(2,1)} %param.14) | copy-start | bytes 98308
  7.2 211.4 %all-gather.2.cloned.1.call-start = ((), (), s32[]{:S(2)}) async-start(), calls=%async_computation | async-start | bytes 1081344 | tf_op jit(solution)/shard_map/all_gather | solution.py:52
  7.9 537.5 %all-reduce.3.cloned.1.call-start = ((), (), s32[]{:S(2)}) async-start(), calls=%async_computation.1 | async-start | bytes 2097152 | tf_op jit(solution)/shard_map/psum | solution.py:62
  226.2 3.9 copy-start.5
  240.7 4.0 copy-start.1
  244.7 769.2 %all-reduce.5.cloned.1.call-start = ((), (), s32[]{:S(2)}) async-start(), calls=%async_computation.2 | async-start | bytes 524288 | tf_op jit(solution)/shard_map/psum | solution.py:69
  245.4 300.9 %copy-start.2 = (bf16[4,32,128]{2,1,0:T(8,128)(2,1)S(1)}, bf16[4,32,128]{2,1,0:T(8,128)(2,1)}, u32[]{:S(2)}) copy-start(bf16[4,32,128]{2,1,0:T(8,128)(2,1)} %param.9) | copy-start | bytes 98308
  245.4 301.1 %copy-start.4 = (bf16[128,128]{1,0:T(8,128)(2,1)S(1)}, bf16[128,128]{1,0:T(8,128)(2,1)}, u32[]{:S(2)}) copy-start(bf16[128,128]{1,0:T(8,128)(2,1)} %param.12) | copy-start | bytes 98308
  245.7 301.9 %copy-start.6 = (bf16[128,128]{1,0:T(8,128)(2,1)S(1)}, bf16[128,128]{1,0:T(8,128)(2,1)}, u32[]{:S(2)}) copy-start(bf16[128,128]{1,0:T(8,128)(2,1)} %param.13) | copy-start | bytes 98308
Sparse Core Ops, SparseCore 0:
  10.1 208.4 all-gather.1
  244.8 300.5 all-reduce.2
  551.4 462.4 all-reduce.4
where the time goes:
time: 1020 us
  waiting for transfers between devices  902 us (88%)
  blocking collectives  63.7 us (6%)
  local copies, waits for them, and re-layouts  20.1 us (2%)
  matrix products  17 us (2%)
  between operations  13.9 us (1%)
    psum x1, waiting for transfers between devices, on_device(): total_weights = lax.psum(local_weights, ('row', 'col'))  465 us
    psum x1, waiting for transfers between devices, on_device(): summed = lax.psum(partial_value, 'col')  299 us
    all_gather x1, waiting for transfers between devices, on_device(): grad_all = lax.all_gather(grad_out, 'row', axis=0, tiled=True)  138 us
    all_gather x1, blocking collectives, on_device(): slab_all = lax.all_gather(slab_value, 'col', axis=0, tiled=True)  63.7 us
  transfers between devices with their start and end apart: 3, of which 3 were waited for; matrix products, arithmetic and copies ran while one was open for 1% of the time, Pallas kernels for 0%

commit v1 on v0

v1 whole, which is shorter than its diff:
```python
import functools

import jax
import jax.numpy as jnp
from jax import lax
from jax.experimental import pallas as pl
from jax.experimental.pallas import tpu as pltpu
from jax.sharding import PartitionSpec as P

MESH = pl.DeviceIdType.MESH
F32 = jnp.float32
BF16 = jnp.bfloat16
VMEM = pl.BlockSpec(memory_space=pltpu.VMEM)
SMEM = pl.BlockSpec(memory_space=pltpu.SMEM)


class Here:
    def __init__(self):
        row = lax.axis_index("row")
        col = lax.axis_index("col")
        self.row, self.col = row, col
        self.z, self.y = row // 4, row % 4
        self.x, self.h, self.core = col // 4, (col // 2) % 2, col % 2

    def at(self, z=None, y=None, x=None, h=None, core=None):
        z = self.z if z is None else z
        y = self.y if y is None else y
        x = self.x if x is None else x
        h = self.h if h is None else h
        core = self.core if core is None else core
        return (z * 4 + y, x * 4 + h * 2 + core)


class Sender:
    def __init__(self, send_sems):
        self.send_sems = send_sems
        self.started = []

    def send(self, src, dst, recv_sem, device):
        copy = pltpu.make_async_remote_copy(
            src_ref=src,
            dst_ref=dst,
            send_sem=self.send_sems.at[len(self.started)],
            recv_sem=recv_sem,
            device_id=device,
            device_id_type=MESH,
        )
        copy.start()
        self.started.append(copy)

    def recv(self, dst, recv_sem, device):
        pltpu.make_async_remote_copy(
            src_ref=dst,
            dst_ref=dst,
            send_sem=self.send_sems.at[0],
            recv_sem=recv_sem,
            device_id=device,
            device_id_type=MESH,
        ).wait_recv()

    def finish(self):
        for copy in self.started:
            copy.wait_send()


def greet(peers):
    barrier = pltpu.get_barrier_semaphore()
    for peer in peers:
        pl.semaphore_signal(barrier, inc=1, device_id=peer, device_id_type=MESH)
    return lambda: pl.semaphore_wait(barrier, len(peers))


GATHER_SENDS = 7 + 32 + 15


def gather_kernel(grad_ref, slab_ref, grad_all, slab_all, send_sems, gz, gy, sh, sx, sc):
    me = Here()
    zg, zl = me.z // 4, me.z % 4
    group = [me.at(z=zg * 4 + (zl + d) % 4) for d in (1, 2, 3)]
    across = me.at(z=(1 - zg) * 4 + zl)
    up, down = me.at(y=(me.y + 1) % 4), me.at(y=(me.y + 3) % 4)
    far = me.at(h=1 - me.h)
    ring = [me.at(x=(me.x + d) % 4) for d in (1, 2, 3)]
    twin = me.at(core=1 - me.core)
    ready = greet(group + [across, up, down, far] + ring + [twin])
    ready()
    out = Sender(send_sems)

    def z_of(t):
        side = zg if t < 4 else 1 - zg
        return side * 4 + (zl + 4 - t % 4) % 4

    def block(t, y=None):
        return grad_all.at[z_of(t) * 4 + (me.y if y is None else y)]

    def col_of(u, d, core=None):
        h = me.h if u == 0 else 1 - me.h
        return ((me.x + 4 - d) % 4) * 4 + h * 2 + (me.core if core is None else core)

    own = grad_all.at[me.row]
    slab_own = slab_all.at[me.col]
    out.send(slab_ref, slab_own, sh.at[0], far)
    out.send(grad_ref, own, gz.at[3], across)
    for d in (1, 3, 2):
        out.send(grad_ref, own, gz.at[d - 1], group[d - 1])
    for side, peer in ((0, up), (1, down)):
        out.send(grad_ref, own, gy.at[0, side], peer)
    for d in (1, 3, 2):
        out.send(slab_ref, slab_own, sx.at[0, d - 1], ring[d - 1])
    out.send(slab_ref, slab_own, sc.at[0, 0], twin)
    grad_all[me.row] = grad_ref[...]
    slab_all[me.col] = slab_ref[...]

    below, above, across_y = (me.y + 3) % 4, (me.y + 1) % 4, (me.y + 2) % 4

    def relay(t):
        out.recv(block(t, below), gy.at[t, 0], down)
        half = block(t, below).at[0]
        out.send(half, half, gy.at[t, 2], up)
        out.recv(block(t, above), gy.at[t, 1], up)
        half = block(t, above).at[1]
        out.send(half, half, gy.at[t, 3], down)

    def slab_round(u):
        for d in (1, 3, 2):
            spot = slab_all.at[col_of(u, d)]
            out.recv(spot, sx.at[u, d - 1], ring[0])
            out.send(spot, spot, sc.at[u, d], twin)

    order = (0, 1, 3, 2, 4, 5, 7, 6)
    for n, t in enumerate(order):
        if t > 0:
            out.recv(block(t), gz.at[t - 1], across)
            if t == 4:
                for d in (1, 3, 2):
                    out.send(block(t), block(t), gz.at[3 + d], group[d - 1])
            out.send(block(t), block(t), gy.at[t, 0], up)
            out.send(block(t), block(t), gy.at[t, 1], down)
            relay(order[n - 1])
        if n == 2:
            slab_round(0)
        if n == 5:
            spot = slab_all.at[col_of(1, 0)]
            out.recv(spot, sh.at[0], far)
            for d in (1, 3, 2):
                out.send(spot, spot, sx.at[1, d - 1], ring[d - 1])
            out.send(spot, spot, sc.at[1, 0], twin)
    relay(order[-1])
    slab_round(1)
    for t in range(8):
        out.recv(block(t, across_y).at[0], gy.at[t, 2], down)
        out.recv(block(t, across_y).at[1], gy.at[t, 3], up)
    for u in range(2):
        for d in range(4):
            spot = slab_all.at[col_of(u, d, 1 - me.core)]
            out.recv(spot, sc.at[u, d], twin)
    out.finish()


def gather(grad_out, pair_slab):
    grad_all, slab_all = pl.pallas_call(
        gather_kernel,
        out_shape=(
            jax.ShapeDtypeStruct((32, 2, 64, 128), BF16),
            jax.ShapeDtypeStruct((16, 4, 32, 128), BF16),
        ),
        in_specs=[VMEM, VMEM],
        out_specs=(VMEM, VMEM),
        scratch_shapes=[
            pltpu.SemaphoreType.DMA((GATHER_SENDS,)),
            pltpu.SemaphoreType.DMA((7,)),
            pltpu.SemaphoreType.DMA((8, 4)),
            pltpu.SemaphoreType.DMA((1,)),
            pltpu.SemaphoreType.DMA((2, 3)),
            pltpu.SemaphoreType.DMA((2, 4)),
        ],
        compiler_params=pltpu.CompilerParams(collective_id=0, has_side_effects=True),
        name="gather",
    )(grad_out, pair_slab)
    return grad_all.reshape(4096, 128), slab_all.reshape(2048, 128)


def key_mask(mask_ref, base):
    spots = lax.broadcasted_iota(jnp.int32, (32, 128), 0)
    flags = jnp.zeros((32, 128), F32)
    for k in range(32):
        flags = jnp.where(spots == k, mask_ref[base + k].astype(F32), flags)
    return flags


def gates(rows, both, flags):
    product = jnp.dot(rows, both, preferred_element_type=F32)
    linear, sigmoid = product[:, :128], jax.nn.sigmoid(product[:, 128:])
    to_linear = flags * sigmoid
    return to_linear * linear, to_linear, to_linear * linear * (1.0 - sigmoid)


def local_kernel(
    grad_ref, slab_ref, pair_ref, wal, wag, wbl, wbg, mask_slab, mask_res,
    grad_pair, partial, weights,
    wide, both_a, both_b, slab_value, slab_lin, slab_gate, pair_value, pair_lin, pair_gate, both_d,
):
    row, col = lax.axis_index("row"), lax.axis_index("col")
    both_a[:, :128], both_a[:, 128:] = wal[...], wag[...]
    both_b[:, :128], both_b[:, 128:] = wbl[...], wbg[...]
    keys = key_mask(mask_res, row * 32)

    def forward(n, first, mask, source, both, value, to_lin, to_gate):
        rows = pl.ds(pl.multiple_of(n * 256, 256), 256)
        flags = jnp.concatenate(
            [keys * mask[first + n * 8 + m].astype(F32) for m in range(8)], axis=0
        )
        val, lin, gate = gates(source[rows, :], both[...], flags)
        value[rows, :] = val.astype(BF16).astype(F32)
        to_lin[rows, :] = lin
        to_gate[rows, :] = gate

    @pl.loop(0, 8)
    def _(n):
        forward(n, 0, mask_slab, slab_ref, both_a, slab_value, slab_lin, slab_gate)
        forward(n, col * 64, mask_res, pair_ref, both_b, pair_value, pair_lin, pair_gate)
        rows = pl.ds(pl.multiple_of(n * 512, 512), 512)
        wide[rows, :] = grad_ref[rows, :].astype(F32)

    def contract(scalar_row, vectors):
        def step(s, acc):
            lanes = [vectors[pl.ds(pl.multiple_of(s * 32 + t * 8, 8), 8), :] for t in range(4)]
            new = []
            for m in range(8):
                factor = wide[pl.ds(scalar_row(s, m), 8, stride=0), :]
                new += [acc[m * 4 + t] + factor * lanes[t] for t in range(4)]
            return tuple(new)

        start = tuple(jnp.zeros((8, 128), F32) for _ in range(32))
        return jnp.concatenate(lax.fori_loop(0, 64, step, start, unroll=4), axis=0)

    def backward(rows, grad, source, to_lin, to_gate):
        both_d[:, :128] = (grad * to_lin[rows, :]).astype(BF16)
        both_d[:, 128:] = (grad * to_gate[rows, :]).astype(BF16)
        return lax.dot_general(
            source[rows, :], both_d[...], (((0,), (0,)), ((), ())), preferred_element_type=F32
        )

    weights[...] = jnp.zeros_like(weights)

    def add_weights(first, both):
        weights[first : first + 128, :] += both[:, :128]
        weights[first + 128 : first + 256, :] += both[:, 128:]

    @pl.loop(0, 8)
    def _(n):
        rows = pl.ds(pl.multiple_of(n * 256, 256), 256)
        grad = contract(lambda s, m: s * 64 + n * 8 + m, slab_value)
        add_weights(256, backward(rows, grad, pair_ref, pair_lin, pair_gate))
        grad_pair[rows, :] = lax.dot_general(
            both_d[...], both_b[...], (((1,), (1,)), ((), ())), preferred_element_type=F32
        ).astype(BF16)
        grad = contract(lambda s, m: (n * 8 + m) * 64 + s, pair_value)
        for m in range(2):
            owner = n * 2 + m
            partial[owner % 2, owner // 2] = grad[m * 128 : (m + 1) * 128, :].astype(BF16)
        add_weights(0, backward(rows, grad, slab_ref, slab_lin, slab_gate))


def local(grad_all, slab_all, pair_full, weights, mask_slab, mask_residue):
    wide = pltpu.VMEM((2048, 128), F32)
    return pl.pallas_call(
        local_kernel,
        out_shape=(
            jax.ShapeDtypeStruct((2048, 128), BF16),
            jax.ShapeDtypeStruct((2, 8, 128, 128), BF16),
            jax.ShapeDtypeStruct((512, 128), F32),
        ),
        in_specs=[VMEM] * 7 + [SMEM] * 2,
        out_specs=(VMEM,) * 3,
        scratch_shapes=[
            pltpu.VMEM((4096, 128), F32),
            pltpu.VMEM((128, 256), BF16),
            pltpu.VMEM((128, 256), BF16),
            wide, wide, wide, wide, wide, wide,
            pltpu.VMEM((256, 256), BF16),
        ],
        name="local",
    )(grad_all, slab_all, pair_full.reshape(2048, 128), *weights, mask_slab, mask_residue)


REDUCE_SENDS = 1 + 3 + 1 + 1 + 3 + 3 + 15 + 3 + 3 + 1


def reduce_kernel(
    partial, weights, slab_ref, wal, wag, mask_slab, mask_res,
    grad_slab, total,
    both, to_lin, to_gate, both_d,
    p_core, p_one, p_x, p_two, p_h,
    w_core, w_one, w_x, w_two, w_y, w_three, w_z,
    send_sems, p_sems, c_sem, x_sems, y_sems, z_sems, yg_sems, xg_sems, cg_sem,
):
    me = Here()
    depth = me.h * 8 + me.z

    def deep(d):
        place = (depth + d) % 16
        return me.at(z=place % 8, h=place // 8)

    twin = me.at(core=1 - me.core)
    far = me.at(h=1 - me.h)
    xs = [me.at(x=(me.x + d) % 4) for d in (1, 2, 3)]
    ys = [me.at(y=(me.y + d) % 4) for d in (1, 2, 3)]
    zs = [deep(d) for d in range(1, 16)]
    ready = greet([twin] + xs + ys + zs)

    both[:, :128], both[:, 128:] = wal[...], wag[...]
    keys = key_mask(mask_res, me.row * 32)
    flags = jnp.concatenate([keys * mask_slab[me.col * 4 + m].astype(F32) for m in range(4)], axis=0)
    _, lin, gate = gates(slab_ref[...], both[...], flags)
    to_lin[...] = lin
    to_gate[...] = gate

    ready()
    out = Sender(send_sems)
    out.send(weights.at[1 - me.core], w_core, c_sem.at[0], twin)
    out.send(partial.at[1 - me.core], p_core, p_sems.at[0], twin)

    out.recv(w_core, c_sem.at[0], twin)
    w_one[...] = weights[me.core] + w_core[...]
    for d in (1, 3, 2):
        out.send(w_one.at[(me.x + d) % 4], w_x.at[d - 1], x_sems.at[d - 1], xs[d - 1])
    out.recv(p_core, p_sems.at[0], twin)
    p_one[...] = (partial[me.core].astype(F32) + p_core[...].astype(F32)).astype(BF16)
    for d in (1, 3, 2):
        spot = pl.ds(((me.x + d) % 4) * 2, 2)
        out.send(p_one.at[spot], p_x.at[d - 1], p_sems.at[d], xs[d - 1])

    sums = w_one[me.x]
    for d in (1, 3, 2):
        out.recv(w_x.at[d - 1], x_sems.at[d - 1], twin)
        sums = sums + w_x[d - 1]
    w_two[...] = sums
    for d in (1, 3, 2):
        out.send(w_two.at[(me.y + d) % 4], w_y.at[d - 1], y_sems.at[d - 1], ys[d - 1])

    sums = p_one[pl.ds(me.x * 2, 2)].astype(F32)
    for d in (1, 3, 2):
        out.recv(p_x.at[d - 1], p_sems.at[d], twin)
        sums = sums + p_x[d - 1].astype(F32)
    p_two[...] = sums.astype(BF16)
    out.send(p_two.at[1 - me.h], p_h, p_sems.at[4], far)

    sums = w_two[me.y]
    for d in (1, 3, 2):
        out.recv(w_y.at[d - 1], y_sems.at[d - 1], twin)
        sums = sums + w_y[d - 1]
    w_three[...] = sums
    w_z[depth] = sums
    for d in (8, 7, 9, 6, 10, 5, 11, 4, 12, 3, 13, 2, 14, 1, 15):
        out.send(w_three, w_z.at[depth], z_sems.at[d - 1], zs[d - 1])

    for d in (1, 15, 2, 14, 3, 13, 4, 12, 5, 11, 6, 10, 7, 9, 8):
        out.recv(w_z.at[(depth + 16 - d) % 16], z_sems.at[d - 1], twin)
    sums = w_z[0]
    for n in range(1, 16):
        sums = sums + w_z[n]
    total[me.core, me.x, me.y] = sums * (1.0 / 1024.0)
    spot = total.at[me.core, me.x, me.y]
    for d in (1, 3, 2):
        out.send(spot, spot, yg_sems.at[d - 1], ys[d - 1])

    out.recv(p_h, p_sems.at[4], far)
    grad = (p_two[me.h].astype(F32) + p_h[...].astype(F32))
    both_d[:, :128] = (grad * to_lin[...]).astype(BF16)
    both_d[:, 128:] = (grad * to_gate[...]).astype(BF16)
    grad_slab[...] = lax.dot_general(
        both_d[...], both[...], (((1,), (1,)), ((), ())), preferred_element_type=F32
    ).astype(BF16)

    for d in (1, 3, 2):
        out.recv(total.at[me.core, me.x, (me.y + 4 - d) % 4], yg_sems.at[d - 1], twin)
    spot = total.at[me.core, me.x]
    for d in (1, 3, 2):
        out.send(spot, spot, xg_sems.at[d - 1], xs[d - 1])
    for d in (1, 3, 2):
        out.recv(total.at[me.core, (me.x + 4 - d) % 4], xg_sems.at[d - 1], twin)
    spot = total.at[me.core]
    out.send(spot, spot, cg_sem.at[0], twin)
    out.recv(total.at[1 - me.core], cg_sem.at[0], twin)
    out.finish()


def reduce(partial, weights, pair_slab, w_a_lin, w_a_gate, mask_slab, mask_residue):
    dma = pltpu.SemaphoreType.DMA
    grad_slab, total = pl.pallas_call(
        reduce_kernel,
        out_shape=(
            jax.ShapeDtypeStruct((128, 128), BF16),
            jax.ShapeDtypeStruct((2, 4, 4, 16, 128), F32),
        ),
        in_specs=[VMEM] * 5 + [SMEM] * 2,
        out_specs=(VMEM, VMEM),
        scratch_shapes=[
            pltpu.VMEM((128, 256), BF16),
            pltpu.VMEM((128, 128), F32),
            pltpu.VMEM((128, 128), F32),
            pltpu.VMEM((128, 256), BF16),
            pltpu.VMEM((8, 128, 128), BF16),
            pltpu.VMEM((8, 128, 128), BF16),
            pltpu.VMEM((3, 2, 128, 128), BF16),
            pltpu.VMEM((2, 128, 128), BF16),
            pltpu.VMEM((128, 128), BF16),
            pltpu.VMEM((4, 4, 16, 128), F32),
            pltpu.VMEM((4, 4, 16, 128), F32),
            pltpu.VMEM((3, 4, 16, 128), F32),
            pltpu.VMEM((4, 16, 128), F32),
            pltpu.VMEM((3, 16, 128), F32),
            pltpu.VMEM((16, 128), F32),
            pltpu.VMEM((16, 16, 128), F32),
            dma((REDUCE_SENDS,)), dma((5,)), dma((1,)), dma((3,)), dma((3,)), dma((15,)),
            dma((3,)), dma((3,)), dma((1,)),
        ],
        compiler_params=pltpu.CompilerParams(collective_id=1, has_side_effects=True),
        name="reduce",
    )(
        partial,
        weights.reshape(2, 4, 4, 16, 128),
        pair_slab.reshape(128, 128),
        w_a_lin,
        w_a_gate,
        mask_slab,
        mask_residue,
    )
    return grad_slab.reshape(4, 32, 128), total.reshape(4, 128, 128)


def on_device(
    pair_slab, pair_full, grad_out, w_a_lin, w_a_gate, w_b_lin, w_b_gate, mask_slab, mask_residue
):
    grad_all, slab_all = gather(grad_out, pair_slab)
    grad_pair, partial, weights = local(
        grad_all, slab_all, pair_full, (w_a_lin, w_a_gate, w_b_lin, w_b_gate), mask_slab, mask_residue
    )
    grad_slab, grad_weights = reduce(
        partial, weights, pair_slab, w_a_lin, w_a_gate, mask_slab, mask_residue
    )
    return (grad_slab, grad_pair.reshape(64, 32, 128), grad_weights)


def solution(mesh):
    return jax.shard_map(
        on_device,
        mesh=mesh,
        in_specs=(
            P("col", "row", None),
            P("col", "row", None),
            P("row", "col", None),
            P(),
            P(),
            P(),
            P(),
            P(),
            P(),
        ),
        out_specs=(P("col", "row", None), P("col", "row", None), P()),
        check_vma=False,
    )
```

time: 1020 us -> 106 us (0.10)
  waiting for transfers between devices: 902 us -> 0 us
  Pallas kernels: 0 us -> 102 us
  blocking collectives: 63.7 us -> 0 us
  local copies, waits for them, and re-layouts: 20.1 us -> 3.04 us
  matrix products: 17 us -> 0 us
  between operations: 13.9 us -> 0.65 us
    psum x2 -> x0, waiting for transfers between devices: 764 us -> none  [the longest x1 465 us: on_device(): total_weights = lax.psum(local_weights, ('row', 'col'))]
    all_gather x1 -> x0, waiting for transfers between devices: 138 us -> none  [on_device(): grad_all = lax.all_gather(grad_out, 'row', axis=0, tiled=True)]
    pallas_call x0 -> x3, Pallas kernels: none -> 102 us  [the longest x1 44.4 us: gather(): pl.pallas_call(gather_kernel, out_shape=(jax.ShapeDtypeStruct((32, 2, 64,...]
    all_gather x1 -> x0, blocking collectives: 63.7 us -> none  [on_device(): slab_all = lax.all_gather(slab_value, 'col', axis=0, tiled=True)]
    dot_general x14 -> x0, matrix products: 17 us -> none  [the longest x2 4.12 us: forward_gate(): jnp.einsum('rkd,dc->rkc', pair, w_gate, preferred_element_type=jnp.float32)]
  transfers between devices with their start and end apart: 3 -> 0, of which waited for: 3 -> 0; matrix products, arithmetic and copies ran while one was open for 1% -> 0% of each run, Pallas kernels for 0% -> 0%
where the time goes in v1:
time: 106 us
  Pallas kernels  102 us (96%)
  local copies, waits for them, and re-layouts  3.04 us (3%)
    pallas_call x1, Pallas kernels, gather(): pl.pallas_call(gather_kernel, out_shape=(jax.ShapeDtypeStruct((32, 2, 64,...  44.4 us
    pallas_call x1, Pallas kernels, reduce(): pl.pallas_call(reduce_kernel, out_shape=(jax.ShapeDtypeStruct((128, 128),...  39 us
    pallas_call x1, Pallas kernels, local(): pl.pallas_call(local_kernel, out_shape=(jax.ShapeDtypeStruct((2048, 128),...  18.9 us
    unnamed x2, local copies, waits for them, and re-layouts  3.04 us

profile of v1, /device:TPU:1, one launch (start us, length us, event | category | flops | bytes accessed | tf_op | source)
XLA Modules:
  0.0 105.9 jit_solution(7515702566604605014)
XLA Ops:
  0.6 44.4 %gather.1 = (bf16[32,2,64,128]{3,2,1,0:T(8,128)(2,1)}, bf16[16,4,32,128]{3,2,1,0:T(8,128)(2,1)}) custom-call(bf16[2,64,128]{2,1,0:T(8,128)(2,1)} %grad_ref.1, bf16[4,32,128]{2,1,0:T(8,128)(2,1)} %slab_ref.1), custom_call_target="tpu_custom_call" | custom-call | tf_op jit(solution)/shard_map/gather/pallas_call | solution.py:161
  45.0 18.9 %local.1 = (bf16[2048,128]{1,0:T(8,128)(2,1)}, bf16[2,8,128,128]{3,2,1,0:T(8,128)(2,1)}, f32[512,128]{1,0:T(8,128)}) custom-call(bf16[4096,128]{1,0:T(8,128)(2,1)} %bitcast.8, bf16[2048,128]{1,0:T(8,128)(2,1)} %bitcast.10, bf16[2048,128]{1,0:T(8,128)(2,1)} %bitcast.9, bf16[128,128]{1,0:T(8,128)(2,1)} %wal.3, bf16[128,128]{1,0:T(8,128)(2,1)} %wag.3, ...), custom_call_target="tpu_custom_call" | custom-call | tf_op jit(solution)/shard_map/local/pallas_call | solution.py:267
  63.9 39.0 %reduce.1 = (bf16[128,128]{1,0:T(8,128)(2,1)}, f32[2,4,4,16,128]{4,3,2,1,0:T(8,128)}) custom-call(bf16[2,8,128,128]{3,2,1,0:T(8,128)(2,1)} %get-tuple-element.12.partial, f32[2,4,4,16,128]{4,3,2,1,0:T(8,128)} %bitcast.11, bf16[128,128]{1,0:T(8,128)(2,1)} %bitcast.13, bf16[128,128]{1,0:T(8,128)(2,1)} %wal.3, bf16[128,128]{1,0:T(8,128)(2,1)} %wag.3, ...), custom_call_target="tpu_custom_call" | custom-call | tf_op jit(solution)/shard_map/reduce/pallas_call | solution.py:391
  102.9 1.4 %copy.14 = bf16[4,32,128]{2,1,0:T(8,128)(2,1)} copy(bf16[4,32,128]{2,1,0:T(8,128)(2,1)} %bitcast.14) | data formatting | bytes 65536
  104.2 1.7 %copy.15 = f32[4,128,128]{2,1,0:T(8,128)} copy(f32[4,128,128]{2,1,0:T(8,128)} %bitcast.12) | data formatting | bytes 524288

commit v2 on v0

v2 whole, which is shorter than its diff:
```python
import jax
import jax.numpy as jnp
from jax import lax
from jax.experimental import pallas as pl
from jax.experimental.pallas import tpu as pltpu
from jax.sharding import PartitionSpec as P

MESH = pl.DeviceIdType.MESH
F32 = jnp.float32
BF16 = jnp.bfloat16
VMEM = pl.BlockSpec(memory_space=pltpu.VMEM)
SMEM = pl.BlockSpec(memory_space=pltpu.SMEM)


class Here:
    def __init__(self):
        row = lax.axis_index("row")
        col = lax.axis_index("col")
        self.row, self.col = row, col
        self.z, self.y = row // 4, row % 4
        self.x, self.h, self.core = col // 4, (col // 2) % 2, col % 2

    def at(self, z=None, y=None, x=None, h=None, core=None):
        z = self.z if z is None else z
        y = self.y if y is None else y
        x = self.x if x is None else x
        h = self.h if h is None else h
        core = self.core if core is None else core
        return (z * 4 + y, x * 4 + h * 2 + core)


class Sender:
    def __init__(self, send_sems, anyone):
        self.send_sems, self.anyone = send_sems, anyone
        self.started = []

    def send(self, src, dst, recv_sem, device):
        copy = pltpu.make_async_remote_copy(
            src_ref=src,
            dst_ref=dst,
            send_sem=self.send_sems.at[len(self.started)],
            recv_sem=recv_sem,
            device_id=device,
            device_id_type=MESH,
        )
        copy.start()
        self.started.append(copy)

    def recv(self, dst, recv_sem):
        pltpu.make_async_remote_copy(
            src_ref=dst,
            dst_ref=dst,
            send_sem=self.send_sems.at[0],
            recv_sem=recv_sem,
            device_id=self.anyone,
            device_id_type=MESH,
        ).wait_recv()

    def finish(self):
        for copy in self.started:
            copy.wait_send()


def key_mask(mask_ref, base):
    spots = lax.broadcasted_iota(jnp.int32, (32, 128), 0)
    flags = jnp.zeros((32, 128), F32)
    for k in range(32):
        flags = jnp.where(spots == k, mask_ref[base + k].astype(F32), flags)
    return flags


def gates(rows, both, flags):
    product = jnp.dot(rows, both, preferred_element_type=F32)
    linear, sigmoid = product[:, :128], jax.nn.sigmoid(product[:, 128:])
    to_linear = flags * sigmoid
    return to_linear * linear, to_linear, to_linear * linear * (1.0 - sigmoid)


SENDS = 7 + 24 + 15 + 5 + 32 + 15 + 1
NEAR = (1, 3, 2)
XY = tuple((dx, dy) for dx in range(4) for dy in range(4))[1:]


def whole_kernel(
    grad_ref, slab_own_ref, pair_ref, wal, wag, wbl, wbg, mask_slab, mask_res,
    grad_slab, grad_pair, total,
    grad_all, slab_all, wide,
    both_a, both_b, slab_value, slab_lin, slab_gate, pair_value, pair_lin, pair_gate,
    slab_grad, pair_grad, both_d, both_s, sum_a, sum_b, partial,
    p_core, p_one, p_x, p_two, p_h,
    weights, w_core, w_one, w_xy, w_two, w_z,
    send_sems, gz, gy, sh, sx, sc, p_sems, c_sem, xy_sems, z_sems, xyg_sems, cg_sem,
):
    me = Here()
    zg, zl = me.z // 4, me.z % 4
    depth = me.h * 8 + me.z

    def deep(d):
        place = (depth + d) % 16
        return me.at(z=place % 8, h=place // 8)

    group = [me.at(z=zg * 4 + (zl + d) % 4) for d in (1, 2, 3)]
    across = me.at(z=(1 - zg) * 4 + zl)
    ys = [me.at(y=(me.y + d) % 4) for d in (1, 2, 3)]
    xs = [me.at(x=(me.x + d) % 4) for d in (1, 2, 3)]
    xys = [me.at(x=(me.x + dx) % 4, y=(me.y + dy) % 4) for dx, dy in XY]
    zs = [deep(d) for d in range(1, 16)]
    far = me.at(h=1 - me.h)
    twin = me.at(core=1 - me.core)

    peers = [twin] + xys + zs
    barrier = pltpu.get_barrier_semaphore()
    for peer in peers:
        pl.semaphore_signal(barrier, inc=1, device_id=peer, device_id_type=MESH)

    both_a[:, :128], both_a[:, 128:] = wal[...], wag[...]
    both_b[:, :128], both_b[:, 128:] = wbl[...], wbg[...]
    keys = key_mask(mask_res, me.row * 32)

    def forward(n, first, mask, rows_ref, both, value, to_lin, to_gate):
        rows = pl.ds(pl.multiple_of(n * 256, 256), 256)
        flags = jnp.concatenate(
            [keys * mask[first + n * 8 + m].astype(F32) for m in range(8)], axis=0
        )
        val, lin, gate = gates(rows_ref(n), both[...], flags)
        value[rows, :] = val.astype(BF16).astype(F32)
        to_lin[rows, :] = lin
        to_gate[rows, :] = gate

    @pl.loop(0, 8)
    def _(n):
        rows = pl.ds(pl.multiple_of(n * 256, 256), 256)
        forward(n, me.col * 64, mask_res, lambda n: pair_ref[rows, :], both_b, pair_value, pair_lin, pair_gate)

    sum_a[...] = jnp.zeros_like(sum_a)
    sum_b[...] = jnp.zeros_like(sum_b)
    pl.semaphore_wait(barrier, len(peers))
    out = Sender(send_sems, twin)

    def z_of(t):
        side = zg if t < 4 else 1 - zg
        return side * 4 + (zl + 4 - t % 4) % 4

    def block(t, y=None):
        return grad_all.at[z_of(t) * 4 + (me.y if y is None else y)]

    def col_of(u, d, core=None):
        h = me.h if u == 0 else 1 - me.h
        return ((me.x + 4 - d) % 4) * 4 + h * 2 + (me.core if core is None else core)

    own = grad_all.at[me.row]
    slab_own = slab_all.at[me.col]
    out.send(slab_own_ref, slab_own, sh.at[0], far)
    out.send(grad_ref, own, gz.at[3], across)
    for d in NEAR:
        out.send(grad_ref, own, gz.at[d - 1], group[d - 1])
    for d in NEAR:
        out.send(grad_ref, own, gy.at[0, d - 1], ys[d - 1])
    for d in NEAR:
        out.send(slab_own_ref, slab_own, sx.at[0, d - 1], xs[d - 1])
    out.send(slab_own_ref, slab_own, sc.at[0, 0], twin)
    grad_all[me.row] = grad_ref[...]
    slab_all[me.col] = slab_own_ref[...]

    def spread(t):
        out.recv(block(t), gz.at[t - 1])
        if t == 4:
            for d in NEAR:
                out.send(block(t), block(t), gz.at[3 + d], group[d - 1])
        for d in NEAR:
            out.send(block(t), block(t), gy.at[t, d - 1], ys[d - 1])

    def slab_round(u):
        for d in NEAR:
            spot = slab_all.at[col_of(u, d)]
            out.recv(spot, sx.at[u, d - 1])
            out.send(spot, spot, sc.at[u, d], twin)

    def contract(scalar_rows, vectors, vector_row, steps, start, unroll):
        def step(s, acc):
            acc = list(acc)
            for scalar_row, base in zip(scalar_rows, vector_row):
                first = base(s)
                lanes = [vectors[pl.ds(pl.multiple_of(first + t * 8, 8), 8), :] for t in range(4)]
                for m in range(8):
                    factor = wide[pl.ds(scalar_row(s, m), 8, stride=0), :]
                    for t in range(4):
                        acc[m * 4 + t] = acc[m * 4 + t] + factor * lanes[t]
            return tuple(acc)

        return jnp.concatenate(lax.fori_loop(0, steps, step, start, unroll=unroll), axis=0)

    zeros = tuple(jnp.zeros((8, 128), F32) for _ in range(32))

    def slab_sum(t):
        for d in NEAR:
            out.recv(block(t, (me.y + 4 - d) % 4), gy.at[t, d - 1])
        z = z_of(t)
        wide[pl.ds(pl.multiple_of(z * 512, 512), 512), :] = (
            grad_all[pl.ds(z * 4, 4)].reshape(512, 128).astype(F32)
        )
        grad = contract(
            [lambda s, m: (z * 8 + m) * 64 + s], pair_value, [lambda s: s * 32], 64, zeros, 4
        )
        slab_grad[pl.ds(pl.multiple_of(z * 256, 256), 256), :] = grad
        rounded = grad.astype(BF16)
        partial[0, z] = rounded[:128, :]
        partial[1, z] = rounded[128:, :]

    def slab_back(t):
        z = z_of(t)
        rows = pl.ds(pl.multiple_of(z * 256, 256), 256)
        grad = slab_grad[rows, :]
        both_s[:, :128] = (grad * slab_lin[rows, :]).astype(BF16)
        both_s[:, 128:] = (grad * slab_gate[rows, :]).astype(BF16)
        source = slab_all[pl.ds(z * 2, 2)].reshape(256, 128)
        sum_a[...] += lax.dot_general(
            source, both_s[...], (((0,), (0,)), ((), ())), preferred_element_type=F32
        )

    def pair_pass(ts, first, last):
        zz = [z_of(t) for t in ts]

        @pl.loop(0, 8)
        def _(n):
            rows = pl.ds(pl.multiple_of(n * 256, 256), 256)
            start = zeros
            if not first:
                start = tuple(
                    pair_grad[pl.ds(pl.multiple_of(n * 256 + t * 8, 8), 8), :] for t in range(32)
                )
            grad = contract(
                [lambda s, m, z=z: (z * 8 + s) * 64 + n * 8 + m for z in zz],
                slab_value,
                [lambda s, z=z: (z * 8 + s) * 32 for z in zz],
                8,
                start,
                1 if len(ts) > 3 else (2 if len(ts) > 1 else 4),
            )
            if not last:
                pair_grad[rows, :] = grad
            else:
                both_d[rows, :128] = (grad * pair_lin[rows, :]).astype(BF16)
                both_d[rows, 128:] = (grad * pair_gate[rows, :]).astype(BF16)
                sum_b[...] += lax.dot_general(
                    pair_ref[rows, :], both_d[rows, :], (((0,), (0,)), ((), ())),
                    preferred_element_type=F32,
                )

    spread(1)
    spread(3)
    spread(2)
    slab_round(0)
    spread(4)
    slab_sum(0)
    slab_sum(1)
    slab_sum(3)
    spot = slab_all.at[col_of(1, 0)]
    out.recv(spot, sh.at[0])
    for d in NEAR:
        out.send(spot, spot, sx.at[1, d - 1], xs[d - 1])
    out.send(spot, spot, sc.at[1, 0], twin)
    spread(5)
    spread(7)
    slab_sum(2)
    spread(6)
    slab_round(1)
    slab_sum(4)
    for u in range(2):
        for d in range(4):
            out.recv(slab_all.at[col_of(u, d, 1 - me.core)], sc.at[u, d])

    @pl.loop(0, 8)
    def _(n):
        forward(
            n, 0, mask_slab, lambda n: slab_all[pl.ds(n * 2, 2)].reshape(256, 128), both_a,
            slab_value, slab_lin, slab_gate,
        )

    pair_pass((0, 1, 3, 2, 4), True, False)
    for t in (0, 1, 3, 2, 4):
        slab_back(t)
    slab_sum(5)
    slab_sum(7)
    slab_back(5)
    slab_back(7)
    pair_pass((5, 7), False, False)
    slab_sum(6)
    out.send(partial.at[1 - me.core], p_core, p_sems.at[0], twin)
    slab_back(6)
    pair_pass((6,), False, True)

    for n, acc in ((0, sum_a), (1, sum_b)):
        for side in range(2):
            half = acc[:, side * 128 : side * 128 + 128].reshape(8, 16, 128)
            weights[n, pl.ds(side * 8, 8)] = half
    out.send(weights.at[1 - me.core], w_core, c_sem.at[0], twin)

    out.recv(p_core, p_sems.at[0])
    p_one[...] = (partial[me.core].astype(F32) + p_core[...].astype(F32)).astype(BF16)
    for d in NEAR:
        spot = pl.ds(((me.x + d) % 4) * 2, 2)
        out.send(p_one.at[spot], p_x.at[d - 1], p_sems.at[d], xs[d - 1])

    out.recv(w_core, c_sem.at[0])
    w_one[...] = weights[me.core] + w_core[...]
    for n, (dx, dy) in enumerate(XY):
        part = ((me.x + dx) % 4) * 4 + (me.y + dy) % 4
        out.send(w_one.at[part], w_xy.at[n], xy_sems.at[n], xys[n])
    sums = w_one[me.x * 4 + me.y]
    for n in range(15):
        out.recv(w_xy.at[n], xy_sems.at[n])
        sums = sums + w_xy[n]
    w_two[...] = sums
    w_z[depth] = sums
    for d in (8, 7, 9, 6, 10, 5, 11, 4, 12, 3, 13, 2, 14, 1, 15):
        out.send(w_two, w_z.at[depth], z_sems.at[d - 1], zs[d - 1])

    sums = p_one[pl.ds(me.x * 2, 2)].astype(F32)
    for d in NEAR:
        out.recv(p_x.at[d - 1], p_sems.at[d])
        sums = sums + p_x[d - 1].astype(F32)
    p_two[...] = sums
    out.send(p_two.at[1 - me.h], p_h, p_sems.at[4], far)

    @pl.loop(0, 8)
    def _(n):
        rows = pl.ds(pl.multiple_of(n * 256, 256), 256)
        grad_pair[rows, :] = lax.dot_general(
            both_d[rows, :], both_b[...], (((1,), (1,)), ((), ())), preferred_element_type=F32
        ).astype(BF16)

    for d in (1, 15, 2, 14, 3, 13, 4, 12, 5, 11, 6, 10, 7, 9, 8):
        out.recv(w_z.at[(depth + 16 - d) % 16], z_sems.at[d - 1])
    sums = w_z[0]
    for n in range(1, 16):
        sums = sums + w_z[n]
    place = me.x * 4 + me.y
    total[me.core, place] = sums * (1.0 / 1024.0)
    spot = total.at[me.core, place]
    for n, (dx, dy) in enumerate(XY):
        out.send(spot, spot, xyg_sems.at[n], xys[n])

    out.recv(p_h, p_sems.at[4])
    grad = p_two[me.h] + p_h[...]
    rows = pl.ds(pl.multiple_of(me.col * 128, 128), 128)
    both_s[:128, :128] = (grad * slab_lin[rows, :]).astype(BF16)
    both_s[:128, 128:] = (grad * slab_gate[rows, :]).astype(BF16)
    grad_slab[...] = lax.dot_general(
        both_s[:128, :], both_a[...], (((1,), (1,)), ((), ())), preferred_element_type=F32
    ).astype(BF16)

    for n, (dx, dy) in enumerate(XY):
        part = ((me.x + 4 - dx) % 4) * 4 + (me.y + 4 - dy) % 4
        out.recv(total.at[me.core, part], xyg_sems.at[n])
    spot = total.at[me.core]
    out.send(spot, spot, cg_sem.at[0], twin)
    out.recv(total.at[1 - me.core], cg_sem.at[0])
    out.finish()


def on_device(
    pair_slab, pair_full, grad_out, w_a_lin, w_a_gate, w_b_lin, w_b_gate, mask_slab, mask_residue
):
    dma = pltpu.SemaphoreType.DMA
    rows_f32 = pltpu.VMEM((2048, 128), F32)
    grad_slab, grad_pair, total = pl.pallas_call(
        whole_kernel,
        out_shape=(
            jax.ShapeDtypeStruct((128, 128), BF16),
            jax.ShapeDtypeStruct((2048, 128), BF16),
            jax.ShapeDtypeStruct((2, 16, 16, 128), F32),
        ),
        in_specs=[VMEM] * 7 + [SMEM] * 2,
        out_specs=(VMEM,) * 3,
        scratch_shapes=[
            pltpu.VMEM((32, 2, 64, 128), BF16),
            pltpu.VMEM((16, 4, 32, 128), BF16),
            pltpu.VMEM((4096, 128), F32),
            pltpu.VMEM((128, 256), BF16),
            pltpu.VMEM((128, 256), BF16),
            rows_f32, rows_f32, rows_f32, rows_f32, rows_f32, rows_f32, rows_f32, rows_f32,
            pltpu.VMEM((2048, 256), BF16),
            pltpu.VMEM((256, 256), BF16),
            pltpu.VMEM((128, 256), F32),
            pltpu.VMEM((128, 256), F32),
            pltpu.VMEM((2, 8, 128, 128), BF16),
            pltpu.VMEM((8, 128, 128), BF16),
            pltpu.VMEM((8, 128, 128), BF16),
            pltpu.VMEM((3, 2, 128, 128), BF16),
            pltpu.VMEM((2, 128, 128), F32),
            pltpu.VMEM((128, 128), F32),
            pltpu.VMEM((2, 16, 16, 128), F32),
            pltpu.VMEM((16, 16, 128), F32),
            pltpu.VMEM((16, 16, 128), F32),
            pltpu.VMEM((15, 16, 128), F32),
            pltpu.VMEM((16, 128), F32),
            pltpu.VMEM((16, 16, 128), F32),
            dma((SENDS,)), dma((7,)), dma((8, 3)), dma((1,)), dma((2, 3)), dma((2, 4)),
            dma((5,)), dma((1,)), dma((15,)), dma((15,)), dma((15,)), dma((1,)),
        ],
        compiler_params=pltpu.CompilerParams(collective_id=0, has_side_effects=True),
        name="whole",
    )(
        grad_out, pair_slab, pair_full.reshape(2048, 128),
        w_a_lin, w_a_gate, w_b_lin, w_b_gate, mask_slab, mask_residue,
    )
    return (
        grad_slab.reshape(4, 32, 128),
        grad_pair.reshape(64, 32, 128),
        total.reshape(4, 128, 128),
    )


def solution(mesh):
    return jax.shard_map(
        on_device,
        mesh=mesh,
        in_specs=(
            P("col", "row", None),
            P("col", "row", None),
            P("row", "col", None),
            P(),
            P(),
            P(),
            P(),
            P(),
            P(),
        ),
        out_specs=(P("col", "row", None), P("col", "row", None), P()),
        check_vma=False,
    )
```

time: 1020 us -> 85.9 us (0.08)
  waiting for transfers between devices: 902 us -> 0 us
  Pallas kernels: 0 us -> 81 us
  blocking collectives: 63.7 us -> 0 us
  matrix products: 17 us -> 0 us
  local copies, waits for them, and re-layouts: 20.1 us -> 3.99 us
  between operations: 13.9 us -> 0.64 us
    psum x2 -> x0, waiting for transfers between devices: 764 us -> none  [the longest x1 465 us: on_device(): total_weights = lax.psum(local_weights, ('row', 'col'))]
    all_gather x1 -> x0, waiting for transfers between devices: 138 us -> none  [on_device(): grad_all = lax.all_gather(grad_out, 'row', axis=0, tiled=True)]
    pallas_call x0 -> x1, Pallas kernels: none -> 81 us  [on_device(): pl.pallas_call(whole_kernel, out_shape=(jax.ShapeDtypeStruct((128, 128),...]
    all_gather x1 -> x0, blocking collectives: 63.7 us -> none  [on_device(): slab_all = lax.all_gather(slab_value, 'col', axis=0, tiled=True)]
    dot_general x14 -> x0, matrix products: 17 us -> none  [the longest x2 4.12 us: forward_gate(): jnp.einsum('rkd,dc->rkc', pair, w_gate, preferred_element_type=jnp.float32)]
  transfers between devices with their start and end apart: 3 -> 0, of which waited for: 3 -> 0; matrix products, arithmetic and copies ran while one was open for 1% -> 0% of each run, Pallas kernels for 0% -> 0%
where the time goes in v2:
time: 85.9 us; the launch traced here: 85.7 us
  Pallas kernels  81 us (94%)
  local copies, waits for them, and re-layouts  3.99 us (5%)
    pallas_call x1, Pallas kernels, on_device(): pl.pallas_call(whole_kernel, out_shape=(jax.ShapeDtypeStruct((128, 128),...  81 us
    unnamed x5, local copies, waits for them, and re-layouts  3.99 us

profile of v2, /device:TPU:1, one launch (start us, length us, event | category | flops | bytes accessed | tf_op | source)
XLA Modules:
  0.0 85.7 jit_solution(11649266305889152873)
XLA Ops:
  0.6 81.0 %whole.1 = (bf16[128,128]{1,0:T(8,128)(2,1)}, bf16[2048,128]{1,0:T(8,128)(2,1)}, f32[2,16,16,128]{3,2,1,0:T(8,128)}) custom-call(bf16[2,64,128]{2,1,0:T(8,128)(2,1)} %grad_ref.1, bf16[4,32,128]{2,1,0:T(8,128)(2,1)} %slab_own_ref.1, bf16[2048,128]{1,0:T(8,128)(2,1)} %bitcast.4, bf16[128,128]{1,0:T(8,128)(2,1)} %wal.1, bf16[128,128]{1,0:T(8,128)(2,1)} %wag.1, ...), custom_call_target="tpu_custom_call" | custom-call | tf_op jit(solution)/shard_map/whole/pallas_call | solution.py:367
  81.7 1.4 %copy.15 = bf16[4,32,128]{2,1,0:T(8,128)(2,1)} copy(bf16[4,32,128]{2,1,0:T(8,128)(2,1)} %bitcast.7) | data formatting | bytes 65536
  83.1 0.0 copy-start
  83.1 1.9 %copy.16 = bf16[64,32,128]{2,1,0:T(8,128)(2,1)} copy(bf16[64,32,128]{2,1,0:T(8,128)(2,1)} %bitcast.5) | data formatting | bytes 1048576
  85.0 0.0 copy-done
  85.0 0.7 copy.17
Async XLA Ops:
  83.1 1.9 %copy-start = (f32[2,16,16,128]{3,2,1,0:T(8,128)S(1)}, f32[2,16,16,128]{3,2,1,0:T(8,128)}, u32[]{:S(2)}) copy-start(f32[2,16,16,128]{3,2,1,0:T(8,128)} %get-tuple-element.8) | copy-start | bytes 786436

commit v3 on v2

--- a/solution.py
+++ b/solution.py
@@ -34,7 +34,7 @@
         self.send_sems, self.anyone = send_sems, anyone
         self.started = []
 
-    def send(self, src, dst, recv_sem, device):
+    def send(self, src, dst, recv_sem, device, only=None):
         copy = pltpu.make_async_remote_copy(
             src_ref=src,
             dst_ref=dst,
@@ -43,8 +43,11 @@
             device_id=device,
             device_id_type=MESH,
         )
-        copy.start()
-        self.started.append(copy)
+        if only is None:
+            copy.start()
+        else:
+            pl.when(only)(copy.start)
+        self.started.append((copy, only))
 
     def recv(self, dst, recv_sem):
         pltpu.make_async_remote_copy(
@@ -57,8 +60,11 @@
         ).wait_recv()
 
     def finish(self):
-        for copy in self.started:
-            copy.wait_send()
+        for copy, only in self.started:
+            if only is None:
+                copy.wait_send()
+            else:
+                pl.when(only)(copy.wait_send)
 
 
 def key_mask(mask_ref, base):
@@ -76,7 +82,7 @@
     return to_linear * linear, to_linear, to_linear * linear * (1.0 - sigmoid)
 
 
-SENDS = 7 + 24 + 15 + 5 + 32 + 15 + 1
+SENDS = 7 + 24 + 15 + 8 + 8 + 1 + 1 + 15 + 15 + 15 + 16
 NEAR = (1, 3, 2)
 XY = tuple((dx, dy) for dx in range(4) for dy in range(4))[1:]
 
@@ -87,9 +93,9 @@
     grad_all, slab_all, wide,
     both_a, both_b, slab_value, slab_lin, slab_gate, pair_value, pair_lin, pair_gate,
     slab_grad, pair_grad, both_d, both_s, sum_a, sum_b, partial,
-    p_core, p_one, p_x, p_two, p_h,
+    p_core, p_wide, p_one, p_x, p_two, p_h,
     weights, w_core, w_one, w_xy, w_two, w_z,
-    send_sems, gz, gy, sh, sx, sc, p_sems, c_sem, xy_sems, z_sems, xyg_sems, cg_sem,
+    send_sems, gz, gy, sh, sx, sc, pc_sems, px_sems, ph_sem, c_sem, xy_sems, z_sems, xyg_sems, cg_sems,
 ):
     me = Here()
     zg, zl = me.z // 4, me.z % 4
@@ -138,8 +144,7 @@
     out = Sender(send_sems, twin)
 
     def z_of(t):
-        side = zg if t < 4 else 1 - zg
-        return side * 4 + (zl + 4 - t % 4) % 4
+        return (zg + t // 4) % 2 * 4 + (zl + 4 - t % 4) % 4
 
     def block(t, y=None):
         return grad_all.at[z_of(t) * 4 + (me.y if y is None else y)]
@@ -206,6 +211,27 @@
         rounded = grad.astype(BF16)
         partial[0, z] = rounded[:128, :]
         partial[1, z] = rounded[128:, :]
+        out.send(partial.at[1 - me.core, z], p_core.at[z], pc_sems.at[t], twin)
+
+    def slab_push(t):
+        z = z_of(t)
+        out.recv(p_core.at[z], pc_sems.at[t])
+        mine = pl.ds(pl.multiple_of(z * 256 + me.core * 128, 128), 128)
+        both = slab_grad[mine, :] + p_core[z].astype(F32)
+        p_wide[z] = both
+        p_one[z] = both.astype(BF16)
+        d = (z // 2 + 4 - me.x) % 4
+        slot = (d + 3) % 4 % 3
+        out.send(
+            p_one.at[z], p_x.at[slot, z % 2], px_sems.at[slot, z % 2], me.at(x=z // 2), d != 0
+        )
+
+    def slab_owner(h):
+        sums = p_wide[me.x * 2 + h]
+        for d in NEAR:
+            out.recv(p_x.at[d - 1, h], px_sems.at[d - 1, h])
+            sums = sums + p_x[d - 1, h].astype(F32)
+        return sums
 
     def slab_back(t):
         z = z_of(t)
@@ -247,47 +273,60 @@
                     preferred_element_type=F32,
                 )
 
+    def slab_forward(h):
+        for d in range(4):
+            out.recv(slab_all.at[col_of(h, d, 1 - me.core)], sc.at[h, d])
+
+        @pl.loop(0, 4)
+        def _(n):
+            forward(
+                n * 2 + (me.h if h == 0 else 1 - me.h), 0, mask_slab,
+                lambda n: slab_all[pl.ds(n * 2, 2)].reshape(256, 128), both_a,
+                slab_value, slab_lin, slab_gate,
+            )
+
+    odd = (me.z + me.h) % 2
     spread(1)
     spread(3)
     spread(2)
     slab_round(0)
+    slab_sum(0)
     spread(4)
-    slab_sum(0)
+    slab_forward(0)
     slab_sum(1)
-    slab_sum(3)
     spot = slab_all.at[col_of(1, 0)]
     out.recv(spot, sh.at[0])
     for d in NEAR:
         out.send(spot, spot, sx.at[1, d - 1], xs[d - 1])
     out.send(spot, spot, sc.at[1, 0], twin)
+    slab_push(0)
+    slab_sum(3)
     spread(5)
     spread(7)
+    spread(6)
+    slab_push(1)
     slab_sum(2)
-    spread(6)
     slab_round(1)
+    slab_push(3)
+    pair_pass((odd, 2 + odd), True, False)
+    slab_push(2)
     slab_sum(4)
-    for u in range(2):
-        for d in range(4):
-            out.recv(slab_all.at[col_of(u, d, 1 - me.core)], sc.at[u, d])
-
-    @pl.loop(0, 8)
-    def _(n):
-        forward(
-            n, 0, mask_slab, lambda n: slab_all[pl.ds(n * 2, 2)].reshape(256, 128), both_a,
-            slab_value, slab_lin, slab_gate,
-        )
-
-    pair_pass((0, 1, 3, 2, 4), True, False)
-    for t in (0, 1, 3, 2, 4):
+    slab_forward(1)
+    pair_pass((1 - odd, 3 - odd), False, False)
+    for t in range(4):
         slab_back(t)
+    slab_push(4)
     slab_sum(5)
+    slab_back(4)
     slab_sum(7)
     slab_back(5)
+    slab_push(5)
+    pair_pass((4, 5, 7), False, False)
     slab_back(7)
-    pair_pass((5, 7), False, False)
+    slab_push(7)
     slab_sum(6)
-    out.send(partial.at[1 - me.core], p_core, p_sems.at[0], twin)
     slab_back(6)
+    slab_push(6)
     pair_pass((6,), False, True)
 
     for n, acc in ((0, sum_a), (1, sum_b)):
@@ -296,17 +335,13 @@
             weights[n, pl.ds(side * 8, 8)] = half
     out.send(weights.at[1 - me.core], w_core, c_sem.at[0], twin)
 
-    out.recv(p_core, p_sems.at[0])
-    p_one[...] = (partial[me.core].astype(F32) + p_core[...].astype(F32)).astype(BF16)
-    for d in NEAR:
-        spot = pl.ds(((me.x + d) % 4) * 2, 2)
-        out.send(p_one.at[spot], p_x.at[d - 1], p_sems.at[d], xs[d - 1])
-
     out.recv(w_core, c_sem.at[0])
     w_one[...] = weights[me.core] + w_core[...]
     for n, (dx, dy) in enumerate(XY):
         part = ((me.x + dx) % 4) * 4 + (me.y + dy) % 4
         out.send(w_one.at[part], w_xy.at[n], xy_sems.at[n], xys[n])
+    p_two[...] = slab_owner(1 - me.h)
+    out.send(p_two, p_h, ph_sem.at[0], far)
     sums = w_one[me.x * 4 + me.y]
     for n in range(15):
         out.recv(w_xy.at[n], xy_sems.at[n])
@@ -316,12 +351,6 @@
     for d in (8, 7, 9, 6, 10, 5, 11, 4, 12, 3, 13, 2, 14, 1, 15):
         out.send(w_two, w_z.at[depth], z_sems.at[d - 1], zs[d - 1])
 
-    sums = p_one[pl.ds(me.x * 2, 2)].astype(F32)
-    for d in NEAR:
-        out.recv(p_x.at[d - 1], p_sems.at[d])
-        sums = sums + p_x[d - 1].astype(F32)
-    p_two[...] = sums
-    out.send(p_two.at[1 - me.h], p_h, p_sems.at[4], far)
 
     @pl.loop(0, 8)
     def _(n):
@@ -340,9 +369,11 @@
     spot = total.at[me.core, place]
     for n, (dx, dy) in enumerate(XY):
         out.send(spot, spot, xyg_sems.at[n], xys[n])
-
-    out.recv(p_h, p_sems.at[4])
-    grad = p_two[me.h] + p_h[...]
+    out.send(spot, spot, cg_sems.at[15], twin)
+
+    grad = slab_owner(me.h)
+    out.recv(p_h, ph_sem.at[0])
+    grad = grad + p_h[...]
     rows = pl.ds(pl.multiple_of(me.col * 128, 128), 128)
     both_s[:128, :128] = (grad * slab_lin[rows, :]).astype(BF16)
     both_s[:128, 128:] = (grad * slab_gate[rows, :]).astype(BF16)
@@ -350,12 +381,14 @@
         both_s[:128, :], both_a[...], (((1,), (1,)), ((), ())), preferred_element_type=F32
     ).astype(BF16)
 
-    for n, (dx, dy) in enumerate(XY):
-        part = ((me.x + 4 - dx) % 4) * 4 + (me.y + 4 - dy) % 4
-        out.recv(total.at[me.core, part], xyg_sems.at[n])
-    spot = total.at[me.core]
-    out.send(spot, spot, cg_sem.at[0], twin)
-    out.recv(total.at[1 - me.core], cg_sem.at[0])
+    parts = [((me.x + 4 - dx) % 4) * 4 + (me.y + 4 - dy) % 4 for dx, dy in XY]
+    for n in range(15):
+        spot = total.at[me.core, parts[n]]
+        out.recv(spot, xyg_sems.at[n])
+        out.send(spot, spot, cg_sems.at[n], twin)
+    for n in range(15):
+        out.recv(total.at[1 - me.core, parts[n]], cg_sems.at[n])
+    out.recv(total.at[1 - me.core, place], cg_sems.at[15])
     out.finish()
 
 
@@ -386,9 +419,10 @@
             pltpu.VMEM((128, 256), F32),
             pltpu.VMEM((2, 8, 128, 128), BF16),
             pltpu.VMEM((8, 128, 128), BF16),
+            pltpu.VMEM((8, 128, 128), F32),
             pltpu.VMEM((8, 128, 128), BF16),
             pltpu.VMEM((3, 2, 128, 128), BF16),
-            pltpu.VMEM((2, 128, 128), F32),
+            pltpu.VMEM((128, 128), F32),
             pltpu.VMEM((128, 128), F32),
             pltpu.VMEM((2, 16, 16, 128), F32),
             pltpu.VMEM((16, 16, 128), F32),
@@ -397,7 +431,7 @@
             pltpu.VMEM((16, 128), F32),
             pltpu.VMEM((16, 16, 128), F32),
             dma((SENDS,)), dma((7,)), dma((8, 3)), dma((1,)), dma((2, 3)), dma((2, 4)),
-            dma((5,)), dma((1,)), dma((15,)), dma((15,)), dma((15,)), dma((1,)),
+            dma((8,)), dma((3, 2)), dma((1,)), dma((1,)), dma((15,)), dma((15,)), dma((15,)), dma((16,)),
         ],
         compiler_params=pltpu.CompilerParams(collective_id=0, has_side_effects=True),
         name="whole",

time: 85.9 us -> 79.4 us (0.924)
  Pallas kernels: 81 us -> 74.5 us
    pallas_call x1, Pallas kernels: 81 us -> 74.5 us  [on_device(): pl.pallas_call(whole_kernel, out_shape=(jax.ShapeDtypeStruct((128, 128),...]
where the time goes in v3:
time: 79.4 us; the launch traced here: 79.2 us
  Pallas kernels  74.5 us (94%)
  local copies, waits for them, and re-layouts  3.99 us (5%)
    pallas_call x1, Pallas kernels, on_device(): pl.pallas_call(whole_kernel, out_shape=(jax.ShapeDtypeStruct((128, 128),...  74.5 us
    unnamed x5, local copies, waits for them, and re-layouts  3.99 us

profile of v3, /device:TPU:1, one launch (start us, length us, event | category | flops | bytes accessed | tf_op | source)
XLA Modules:
  0.0 79.2 jit_solution(4038668167383051810)
XLA Ops:
  0.6 74.5 %whole.1 = (bf16[128,128]{1,0:T(8,128)(2,1)}, bf16[2048,128]{1,0:T(8,128)(2,1)}, f32[2,16,16,128]{3,2,1,0:T(8,128)}) custom-call(bf16[2,64,128]{2,1,0:T(8,128)(2,1)} %grad_ref.1, bf16[4,32,128]{2,1,0:T(8,128)(2,1)} %slab_own_ref.1, bf16[2048,128]{1,0:T(8,128)(2,1)} %bitcast.4, bf16[128,128]{1,0:T(8,128)(2,1)} %wal.1, bf16[128,128]{1,0:T(8,128)(2,1)} %wag.1, ...), custom_call_target="tpu_custom_call" | custom-call | tf_op jit(solution)/shard_map/whole/pallas_call | solution.py:400
  75.2 1.4 %copy.15 = bf16[4,32,128]{2,1,0:T(8,128)(2,1)} copy(bf16[4,32,128]{2,1,0:T(8,128)(2,1)} %bitcast.7) | data formatting | bytes 65536
  76.5 0.0 copy-start
  76.6 1.9 %copy.16 = bf16[64,32,128]{2,1,0:T(8,128)(2,1)} copy(bf16[64,32,128]{2,1,0:T(8,128)(2,1)} %bitcast.5) | data formatting | bytes 1048576
  78.5 0.0 copy-done
  78.5 0.7 copy.17
Async XLA Ops:
  76.5 1.9 %copy-start = (f32[2,16,16,128]{3,2,1,0:T(8,128)S(1)}, f32[2,16,16,128]{3,2,1,0:T(8,128)}, u32[]{:S(2)}) copy-start(f32[2,16,16,128]{3,2,1,0:T(8,128)} %get-tuple-element.8) | copy-start | bytes 786436

commit v4 on v3

--- a/solution.py
+++ b/solution.py
@@ -8,8 +8,7 @@
 MESH = pl.DeviceIdType.MESH
 F32 = jnp.float32
 BF16 = jnp.bfloat16
-VMEM = pl.BlockSpec(memory_space=pltpu.VMEM)
-SMEM = pl.BlockSpec(memory_space=pltpu.SMEM)
+ANY = pl.BlockSpec(memory_space=pl.ANY)
 
 
 class Here:
@@ -88,8 +87,9 @@
 
 
 def whole_kernel(
-    grad_ref, slab_own_ref, pair_ref, wal, wag, wbl, wbg, mask_slab, mask_res,
-    grad_slab, grad_pair, total,
+    grad_in, slab_in, pair_in, wal, wag, wbl, wbg, mask_slab_in, mask_res_in,
+    grad_slab_out, grad_pair_out, total_out,
+    pair_ref, mask_slab, mask_res, grad_slab, grad_pair, total, in_sems, out_sems,
     grad_all, slab_all, wide,
     both_a, both_b, slab_value, slab_lin, slab_gate, pair_value, pair_lin, pair_gate,
     slab_grad, pair_grad, both_d, both_s, sum_a, sum_b, partial,
@@ -114,13 +114,33 @@
     far = me.at(h=1 - me.h)
     twin = me.at(core=1 - me.core)
 
-    peers = [twin] + xys + zs
+    peers = [twin] + xys + [deep(d) for d in (1, 2, 3, 4, 12, 13, 14, 15)]
     barrier = pltpu.get_barrier_semaphore()
     for peer in peers:
         pl.semaphore_signal(barrier, inc=1, device_id=peer, device_id_type=MESH)
 
-    both_a[:, :128], both_a[:, 128:] = wal[...], wag[...]
-    both_b[:, :128], both_b[:, 128:] = wbl[...], wbg[...]
+    own = grad_all.at[me.row]
+    slab_own = slab_all.at[me.col]
+    loads = [
+        pltpu.make_async_copy(source, target, in_sems.at[n])
+        for n, (source, target) in enumerate(
+            (
+                (mask_res_in, mask_res),
+                (mask_slab_in, mask_slab),
+                (wbl, both_b.at[:, pl.ds(0, 128)]),
+                (wbg, both_b.at[:, pl.ds(128, 128)]),
+                (pair_in, pair_ref),
+                (grad_in, own),
+                (slab_in, slab_own),
+                (wal, both_a.at[:, pl.ds(0, 128)]),
+                (wag, both_a.at[:, pl.ds(128, 128)]),
+            )
+        )
+    ]
+    for load in loads:
+        load.start()
+    for load in loads:
+        load.wait()
     keys = key_mask(mask_res, me.row * 32)
 
     def forward(n, first, mask, rows_ref, both, value, to_lin, to_gate):
@@ -153,19 +173,14 @@
         h = me.h if u == 0 else 1 - me.h
         return ((me.x + 4 - d) % 4) * 4 + h * 2 + (me.core if core is None else core)
 
-    own = grad_all.at[me.row]
-    slab_own = slab_all.at[me.col]
-    out.send(slab_own_ref, slab_own, sh.at[0], far)
-    out.send(grad_ref, own, gz.at[3], across)
+    out.send(own, own, gz.at[3], across)
     for d in NEAR:
-        out.send(grad_ref, own, gz.at[d - 1], group[d - 1])
+        out.send(own, own, gz.at[d - 1], group[d - 1])
     for d in NEAR:
-        out.send(grad_ref, own, gy.at[0, d - 1], ys[d - 1])
+        out.send(own, own, gy.at[0, d - 1], ys[d - 1])
     for d in NEAR:
-        out.send(slab_own_ref, slab_own, sx.at[0, d - 1], xs[d - 1])
-    out.send(slab_own_ref, slab_own, sc.at[0, 0], twin)
-    grad_all[me.row] = grad_ref[...]
-    slab_all[me.col] = slab_own_ref[...]
+        out.send(slab_own, slab_own, sx.at[0, d - 1], xs[d - 1])
+    out.send(slab_own, slab_own, sc.at[0, 0], twin)
 
     def spread(t):
         out.recv(block(t), gz.at[t - 1])
@@ -286,48 +301,47 @@
             )
 
     odd = (me.z + me.h) % 2
-    spread(1)
-    spread(3)
-    spread(2)
+    for t in (1, 3, 2):
+        spread(t)
     slab_round(0)
+    spread(4)
+    out.send(slab_own, slab_own, sh.at[0], far)
     slab_sum(0)
-    spread(4)
     slab_forward(0)
     slab_sum(1)
+    slab_sum(3)
+    spread(5)
+    spread(7)
+    spread(6)
+    slab_push(0)
+    slab_push(1)
+    slab_sum(2)
+    pair_pass((odd, 2 + odd), True, False)
+    slab_push(3)
+    slab_push(2)
+    slab_back(odd)
+    slab_back(2 + odd)
+    slab_sum(4)
     spot = slab_all.at[col_of(1, 0)]
     out.recv(spot, sh.at[0])
     for d in NEAR:
         out.send(spot, spot, sx.at[1, d - 1], xs[d - 1])
     out.send(spot, spot, sc.at[1, 0], twin)
-    slab_push(0)
-    slab_sum(3)
-    spread(5)
-    spread(7)
-    spread(6)
-    slab_push(1)
-    slab_sum(2)
+    slab_sum(5)
+    slab_sum(7)
+    slab_push(4)
+    slab_push(5)
+    slab_sum(6)
+    slab_push(7)
+    pair_pass((4 + odd, 6 + odd), False, False)
+    slab_push(6)
     slab_round(1)
-    slab_push(3)
-    pair_pass((odd, 2 + odd), True, False)
-    slab_push(2)
-    slab_sum(4)
+    slab_back(4 + odd)
+    slab_back(6 + odd)
     slab_forward(1)
-    pair_pass((1 - odd, 3 - odd), False, False)
-    for t in range(4):
-        slab_back(t)
-    slab_push(4)
-    slab_sum(5)
-    slab_back(4)
-    slab_sum(7)
-    slab_back(5)
-    slab_push(5)
-    pair_pass((4, 5, 7), False, False)
-    slab_back(7)
-    slab_push(7)
-    slab_sum(6)
-    slab_back(6)
-    slab_push(6)
-    pair_pass((6,), False, True)
+    for t in (1, 3, 5, 7):
+        slab_back(t - odd)
+    pair_pass((1 - odd, 3 - odd, 5 - odd, 7 - odd), False, True)
 
     for n, acc in ((0, sum_a), (1, sum_b)):
         for side in range(2):
@@ -359,6 +373,9 @@
             both_d[rows, :], both_b[...], (((1,), (1,)), ((), ())), preferred_element_type=F32
         ).astype(BF16)
 
+    stores = [pltpu.make_async_copy(grad_pair, grad_pair_out, out_sems.at[0])]
+    stores[0].start()
+
     for d in (1, 15, 2, 14, 3, 13, 4, 12, 5, 11, 6, 10, 7, 9, 8):
         out.recv(w_z.at[(depth + 16 - d) % 16], z_sems.at[d - 1])
     sums = w_z[0]
@@ -380,6 +397,8 @@
     grad_slab[...] = lax.dot_general(
         both_s[:128, :], both_a[...], (((1,), (1,)), ((), ())), preferred_element_type=F32
     ).astype(BF16)
+    stores.append(pltpu.make_async_copy(grad_slab, grad_slab_out, out_sems.at[1]))
+    stores[1].start()
 
     parts = [((me.x + 4 - dx) % 4) * 4 + (me.y + 4 - dy) % 4 for dx, dy in XY]
     for n in range(15):
@@ -389,7 +408,41 @@
     for n in range(15):
         out.recv(total.at[1 - me.core, parts[n]], cg_sems.at[n])
     out.recv(total.at[1 - me.core, place], cg_sems.at[15])
+    stores.append(pltpu.make_async_copy(total, total_out, out_sems.at[2]))
+    stores[2].start()
     out.finish()
+    for store in stores:
+        store.wait()
+
+
+def settle_kernel(*refs):
+    sources, targets, held, sems = refs[:3], refs[3:6], refs[6:9], refs[9]
+    loads = [pltpu.make_async_copy(sources[n], held[n], sems.at[n]) for n in range(3)]
+    for load in loads:
+        load.start()
+    stores = []
+    for n in range(3):
+        loads[n].wait()
+        stores.append(pltpu.make_async_copy(held[n], targets[n], sems.at[3 + n]))
+        stores[n].start()
+    for store in stores:
+        store.wait()
+
+
+OUTS = (((128, 128), BF16), ((2048, 128), BF16), ((2, 16, 16, 128), F32))
+SHAPES = tuple(jax.ShapeDtypeStruct(*out) for out in OUTS)
+HELD = [pltpu.VMEM(*out) for out in OUTS]
+
+
+def settle(*arrays):
+    return pl.pallas_call(
+        settle_kernel,
+        out_shape=SHAPES,
+        in_specs=[ANY] * 3,
+        out_specs=(ANY,) * 3,
+        scratch_shapes=HELD + [pltpu.SemaphoreType.DMA((6,))],
+        name="settle",
+    )(*arrays)
 
 
 def on_device(
@@ -399,14 +452,16 @@
     rows_f32 = pltpu.VMEM((2048, 128), F32)
     grad_slab, grad_pair, total = pl.pallas_call(
         whole_kernel,
-        out_shape=(
-            jax.ShapeDtypeStruct((128, 128), BF16),
-            jax.ShapeDtypeStruct((2048, 128), BF16),
-            jax.ShapeDtypeStruct((2, 16, 16, 128), F32),
-        ),
-        in_specs=[VMEM] * 7 + [SMEM] * 2,
-        out_specs=(VMEM,) * 3,
+        out_shape=SHAPES,
+        in_specs=[ANY] * 9,
+        out_specs=(ANY,) * 3,
         scratch_shapes=[
+            pltpu.VMEM((2048, 128), BF16),
+            pltpu.SMEM((64,), jnp.int32),
+            pltpu.SMEM((1024,), jnp.int32),
+            *HELD,
+            dma((9,)),
+            dma((3,)),
             pltpu.VMEM((32, 2, 64, 128), BF16),
             pltpu.VMEM((16, 4, 32, 128), BF16),
             pltpu.VMEM((4096, 128), F32),
@@ -439,6 +494,7 @@
         grad_out, pair_slab, pair_full.reshape(2048, 128),
         w_a_lin, w_a_gate, w_b_lin, w_b_gate, mask_slab, mask_residue,
     )
+    grad_slab, grad_pair, total = settle(grad_slab, grad_pair, total)
     return (
         grad_slab.reshape(4, 32, 128),
         grad_pair.reshape(64, 32, 128),

time: 79.4 us -> 70.8 us (0.89)
  Pallas kernels: 74.5 us -> 70 us
  local copies, waits for them, and re-layouts: 3.99 us -> 0 us
    pallas_call x1 -> x2, Pallas kernels: 74.5 us -> 70 us  [the longest x1 68 us: on_device(): pl.pallas_call(whole_kernel, out_shape=SHAPES, in_specs=[ANY] * 9, out_sp...]
    unnamed x5 -> x0, local copies, waits for them, and re-layouts: 3.99 us -> none
where the time goes in v4:
time: 70.8 us; the launch traced here: 70.7 us
  Pallas kernels  70 us (99%)
    pallas_call x1, Pallas kernels, on_device(): pl.pallas_call(whole_kernel, out_shape=SHAPES, in_specs=[ANY] * 9, out_sp...  68 us
    pallas_call x1, Pallas kernels, settle(): pl.pallas_call(settle_kernel, out_shape=SHAPES, in_specs=[ANY] * 3, out_s...  1.99 us

profile of v4, /device:TPU:1, one launch (start us, length us, event | category | flops | bytes accessed | tf_op | source)
XLA Modules:
  0.0 70.7 jit_solution(7441098451645196524)
XLA Ops:
  0.6 68.0 %whole.1 = (bf16[128,128]{1,0:T(8,128)(2,1)}, bf16[2048,128]{1,0:T(8,128)(2,1)}, f32[2,16,16,128]{3,2,1,0:T(8,128)}) custom-call(bf16[2,64,128]{2,1,0:T(8,128)(2,1)} %grad_in.1, bf16[4,32,128]{2,1,0:T(8,128)(2,1)} %slab_in.1, bf16[2048,128]{1,0:T(8,128)(2,1)} %bitcast.4, bf16[128,128]{1,0:T(8,128)(2,1)} %wal.1, bf16[128,128]{1,0:T(8,128)(2,1)} %wag.1, ...), custom_call_target="tpu_custom_call" | custom-call | tf_op jit(solution)/shard_map/whole/pallas_call | solution.py:453
  68.7 2.0 %settle.1 = (bf16[128,128]{1,0:T(8,128)(2,1)}, bf16[2048,128]{1,0:T(8,128)(2,1)}, f32[2,16,16,128]{3,2,1,0:T(8,128)}) custom-call(bf16[128,128]{1,0:T(8,128)(2,1)} %get-tuple-element.9.refs_0_, bf16[2048,128]{1,0:T(8,128)(2,1)} %get-tuple-element.10.refs_1_, f32[2,16,16,128]{3,2,1,0:T(8,128)} %get-tuple-element.11.refs_2_), custom_call_target="tpu_custom_call" | custom-call | tf_op jit(solution)/shard_map/settle/pallas_call | solution.py:438

commit v5 on v4

--- a/solution.py
+++ b/solution.py
@@ -34,6 +34,13 @@
         self.started = []
 
     def send(self, src, dst, recv_sem, device, only=None):
+        copy = self.make(src, dst, recv_sem, device, only)
+        if only is None:
+            copy.start()
+        else:
+            pl.when(only)(copy.start)
+
+    def make(self, src, dst, recv_sem, device, only=None):
         copy = pltpu.make_async_remote_copy(
             src_ref=src,
             dst_ref=dst,
@@ -42,11 +49,8 @@
             device_id=device,
             device_id_type=MESH,
         )
-        if only is None:
-            copy.start()
-        else:
-            pl.when(only)(copy.start)
         self.started.append((copy, only))
+        return copy
 
     def recv(self, dst, recv_sem):
         pltpu.make_async_remote_copy(
@@ -259,10 +263,10 @@
             source, both_s[...], (((0,), (0,)), ((), ())), preferred_element_type=F32
         )
 
-    def pair_pass(ts, first, last):
+    def pair_pass(ts, first, last, begin=0, end=8):
         zz = [z_of(t) for t in ts]
 
-        @pl.loop(0, 8)
+        @pl.loop(begin, end)
         def _(n):
             rows = pl.ds(pl.multiple_of(n * 256, 256), 256)
             start = zeros
@@ -341,21 +345,37 @@
     slab_forward(1)
     for t in (1, 3, 5, 7):
         slab_back(t - odd)
-    pair_pass((1 - odd, 3 - odd, 5 - odd, 7 - odd), False, True)
-
-    for n, acc in ((0, sum_a), (1, sum_b)):
-        for side in range(2):
-            half = acc[:, side * 128 : side * 128 + 128].reshape(8, 16, 128)
-            weights[n, pl.ds(side * 8, 8)] = half
-    out.send(weights.at[1 - me.core], w_core, c_sem.at[0], twin)
-
-    out.recv(w_core, c_sem.at[0])
-    w_one[...] = weights[me.core] + w_core[...]
-    for n, (dx, dy) in enumerate(XY):
-        part = ((me.x + dx) % 4) * 4 + (me.y + dy) % 4
-        out.send(w_one.at[part], w_xy.at[n], xy_sems.at[n], xys[n])
+    hand_over = out.make(weights.at[1 - me.core], w_core, c_sem.at[0], twin)
+    scatter = [
+        out.make(
+            w_one.at[((me.x + dx) % 4) * 4 + (me.y + dy) % 4], w_xy.at[n], xy_sems.at[n], xys[n]
+        )
+        for n, (dx, dy) in enumerate(XY)
+    ]
+
+    def side_sums(n, acc):
+        for part in range(2):
+            half = acc[:, part * 128 : part * 128 + 128].reshape(8, 16, 128)
+            weights[n, pl.ds(part * 8, 8)] = half
+        pl.when(me.core != n)(hand_over.start)
+
+    def side_scatter(n):
+        @pl.when(me.core == n)
+        def _():
+            out.recv(w_core, c_sem.at[0])
+            w_one[...] = weights[n] + w_core[...]
+            for copy in scatter:
+                copy.start()
+
+    last = (1 - odd, 3 - odd, 5 - odd, 7 - odd)
+    side_sums(0, sum_a)
+    pair_pass(last, False, True, 0, 4)
+    side_scatter(0)
     p_two[...] = slab_owner(1 - me.h)
     out.send(p_two, p_h, ph_sem.at[0], far)
+    pair_pass(last, False, True, 4, 8)
+    side_sums(1, sum_b)
+    side_scatter(1)
     sums = w_one[me.x * 4 + me.y]
     for n in range(15):
         out.recv(w_xy.at[n], xy_sems.at[n])

time: 70.8 us -> 67.7 us (0.956)
  Pallas kernels: 70 us -> 66.9 us
    pallas_call x1, Pallas kernels: 68 us -> 64.9 us  [on_device(): pl.pallas_call(whole_kernel, out_shape=SHAPES, in_specs=[ANY] * 9, out_sp...]
where the time goes in v5:
time: 67.7 us; the launch traced here: 67.5 us
  Pallas kernels  66.9 us (99%)
    pallas_call x1, Pallas kernels, on_device(): pl.pallas_call(whole_kernel, out_shape=SHAPES, in_specs=[ANY] * 9, out_sp...  64.9 us
    pallas_call x1, Pallas kernels, settle(): pl.pallas_call(settle_kernel, out_shape=SHAPES, in_specs=[ANY] * 3, out_s...  1.99 us

profile of v5, /device:TPU:1, one launch (start us, length us, event | category | flops | bytes accessed | tf_op | source)
XLA Modules:
  0.0 67.5 jit_solution(3949596542528225799)
XLA Ops:
  0.6 64.9 %whole.1 = (bf16[128,128]{1,0:T(8,128)(2,1)}, bf16[2048,128]{1,0:T(8,128)(2,1)}, f32[2,16,16,128]{3,2,1,0:T(8,128)}) custom-call(bf16[2,64,128]{2,1,0:T(8,128)(2,1)} %grad_in.1, bf16[4,32,128]{2,1,0:T(8,128)(2,1)} %slab_in.1, bf16[2048,128]{1,0:T(8,128)(2,1)} %bitcast.4, bf16[128,128]{1,0:T(8,128)(2,1)} %wal.1, bf16[128,128]{1,0:T(8,128)(2,1)} %wag.1, ...), custom_call_target="tpu_custom_call" | custom-call | tf_op jit(solution)/shard_map/whole/pallas_call | solution.py:473
  65.5 2.0 %settle.1 = (bf16[128,128]{1,0:T(8,128)(2,1)}, bf16[2048,128]{1,0:T(8,128)(2,1)}, f32[2,16,16,128]{3,2,1,0:T(8,128)}) custom-call(bf16[128,128]{1,0:T(8,128)(2,1)} %get-tuple-element.9.refs_0_, bf16[2048,128]{1,0:T(8,128)(2,1)} %get-tuple-element.10.refs_1_, f32[2,16,16,128]{3,2,1,0:T(8,128)} %get-tuple-element.11.refs_2_), custom_call_target="tpu_custom_call" | custom-call | tf_op jit(solution)/shard_map/settle/pallas_call | solution.py:458

commit v6 on v5

--- a/solution.py
+++ b/solution.py
@@ -92,8 +92,8 @@
 
 def whole_kernel(
     grad_in, slab_in, pair_in, wal, wag, wbl, wbg, mask_slab_in, mask_res_in,
-    grad_slab_out, grad_pair_out, total_out,
-    pair_ref, mask_slab, mask_res, grad_slab, grad_pair, total, in_sems, out_sems,
+    grad_slab, grad_pair, total,
+    pair_ref, mask_slab, mask_res, in_sems,
     grad_all, slab_all, wide,
     both_a, both_b, slab_value, slab_lin, slab_gate, pair_value, pair_lin, pair_gate,
     slab_grad, pair_grad, both_d, both_s, sum_a, sum_b, partial,
@@ -189,9 +189,9 @@
     def spread(t):
         out.recv(block(t), gz.at[t - 1])
         if t == 4:
-            for d in NEAR:
+            for d in (2, 1, 3):
                 out.send(block(t), block(t), gz.at[3 + d], group[d - 1])
-        for d in NEAR:
+        for d in (2, 1, 3):
             out.send(block(t), block(t), gy.at[t, d - 1], ys[d - 1])
 
     def slab_round(u):
@@ -393,9 +393,6 @@
             both_d[rows, :], both_b[...], (((1,), (1,)), ((), ())), preferred_element_type=F32
         ).astype(BF16)
 
-    stores = [pltpu.make_async_copy(grad_pair, grad_pair_out, out_sems.at[0])]
-    stores[0].start()
-
     for d in (1, 15, 2, 14, 3, 13, 4, 12, 5, 11, 6, 10, 7, 9, 8):
         out.recv(w_z.at[(depth + 16 - d) % 16], z_sems.at[d - 1])
     sums = w_z[0]
@@ -417,8 +414,6 @@
     grad_slab[...] = lax.dot_general(
         both_s[:128, :], both_a[...], (((1,), (1,)), ((), ())), preferred_element_type=F32
     ).astype(BF16)
-    stores.append(pltpu.make_async_copy(grad_slab, grad_slab_out, out_sems.at[1]))
-    stores[1].start()
 
     parts = [((me.x + 4 - dx) % 4) * 4 + (me.y + 4 - dy) % 4 for dx, dy in XY]
     for n in range(15):
@@ -428,30 +423,22 @@
     for n in range(15):
         out.recv(total.at[1 - me.core, parts[n]], cg_sems.at[n])
     out.recv(total.at[1 - me.core, place], cg_sems.at[15])
-    stores.append(pltpu.make_async_copy(total, total_out, out_sems.at[2]))
-    stores[2].start()
     out.finish()
+
+
+def settle_kernel(*refs):
+    sources, targets, sems = refs[:3], refs[3:6], refs[6]
+    stores = [pltpu.make_async_copy(sources[n], targets[n], sems.at[n]) for n in range(3)]
+    for store in stores:
+        store.start()
     for store in stores:
         store.wait()
 
 
-def settle_kernel(*refs):
-    sources, targets, held, sems = refs[:3], refs[3:6], refs[6:9], refs[9]
-    loads = [pltpu.make_async_copy(sources[n], held[n], sems.at[n]) for n in range(3)]
-    for load in loads:
-        load.start()
-    stores = []
-    for n in range(3):
-        loads[n].wait()
-        stores.append(pltpu.make_async_copy(held[n], targets[n], sems.at[3 + n]))
-        stores[n].start()
-    for store in stores:
-        store.wait()
-
-
 OUTS = (((128, 128), BF16), ((2048, 128), BF16), ((2, 16, 16, 128), F32))
 SHAPES = tuple(jax.ShapeDtypeStruct(*out) for out in OUTS)
-HELD = [pltpu.VMEM(*out) for out in OUTS]
+HELD = tuple(pltpu.VMEM(*out) for out in OUTS)
+VMEM = pl.BlockSpec(memory_space=pltpu.VMEM)
 
 
 def settle(*arrays):
@@ -460,9 +447,9 @@
         out_shape=SHAPES,
         in_specs=[ANY] * 3,
         out_specs=(ANY,) * 3,
-        scratch_shapes=HELD + [pltpu.SemaphoreType.DMA((6,))],
+        scratch_shapes=[pltpu.SemaphoreType.DMA((3,))],
         name="settle",
-    )(*arrays)
+    )(*(pltpu.with_memory_space_constraint(a, pltpu.VMEM) for a in arrays))
 
 
 def on_device(
@@ -472,16 +459,14 @@
     rows_f32 = pltpu.VMEM((2048, 128), F32)
     grad_slab, grad_pair, total = pl.pallas_call(
         whole_kernel,
-        out_shape=SHAPES,
+        out_shape=HELD,
         in_specs=[ANY] * 9,
-        out_specs=(ANY,) * 3,
+        out_specs=(VMEM,) * 3,
         scratch_shapes=[
             pltpu.VMEM((2048, 128), BF16),
             pltpu.SMEM((64,), jnp.int32),
             pltpu.SMEM((1024,), jnp.int32),
-            *HELD,
             dma((9,)),
-            dma((3,)),
             pltpu.VMEM((32, 2, 64, 128), BF16),
             pltpu.VMEM((16, 4, 32, 128), BF16),
             pltpu.VMEM((4096, 128), F32),

time: 67.7 us -> 65.7 us (0.970)
  Pallas kernels: 66.9 us -> 65 us
    pallas_call x1, Pallas kernels: 1.99 us -> 0.91 us  [settle(): pl.pallas_call(settle_kernel, out_shape=SHAPES, in_specs=[ANY] * 3, out_s...]
    pallas_call x1, Pallas kernels: 64.9 us -> 64.1 us  [on_device(): pl.pallas_call(whole_kernel, out_shape=HELD, in_specs=[ANY] * 9, out_spec...]
where the time goes in v6:
time: 65.7 us; the launch traced here: 65.6 us
  Pallas kernels  65 us (99%)
    pallas_call x1, Pallas kernels, on_device(): pl.pallas_call(whole_kernel, out_shape=HELD, in_specs=[ANY] * 9, out_spec...  64.1 us

profile of v6, /device:TPU:1, one launch (start us, length us, event | category | flops | bytes accessed | tf_op | source)
XLA Modules:
  0.0 65.6 jit_solution(1148957391010352785)
XLA Ops:
  0.6 64.1 %whole.1 = (bf16[128,128]{1,0:T(8,128)(2,1)S(1)}, bf16[2048,128]{1,0:T(8,128)(2,1)S(1)}, f32[2,16,16,128]{3,2,1,0:T(8,128)S(1)}) custom-call(bf16[2,64,128]{2,1,0:T(8,128)(2,1)} %grad_in.1, bf16[4,32,128]{2,1,0:T(8,128)(2,1)} %slab_in.1, bf16[2048,128]{1,0:T(8,128)(2,1)} %bitcast.4, bf16[128,128]{1,0:T(8,128)(2,1)} %wal.1, bf16[128,128]{1,0:T(8,128)(2,1)} %wag.1, ...), custom_call_target="tpu_custom_call" | custom-call | tf_op jit(solution)/shard_map/whole/pallas_call | solution.py:460
  64.7 0.9 %settle.1 = (bf16[128,128]{1,0:T(8,128)(2,1)}, bf16[2048,128]{1,0:T(8,128)(2,1)}, f32[2,16,16,128]{3,2,1,0:T(8,128)}) custom-call(bf16[128,128]{1,0:T(8,128)(2,1)S(1)} %get-tuple-element.9.refs_0_, bf16[2048,128]{1,0:T(8,128)(2,1)S(1)} %get-tuple-element.10.refs_1_, f32[2,16,16,128]{3,2,1,0:T(8,128)S(1)} %get-tuple-element.11.refs_2_), custom_call_target="tpu_custom_call" | custom-call | tf_op jit(solution)/shard_map/settle/pallas_call | solution.py:445

commit v7 on v6

--- a/solution.py
+++ b/solution.py
@@ -129,13 +129,13 @@
         pltpu.make_async_copy(source, target, in_sems.at[n])
         for n, (source, target) in enumerate(
             (
+                (slab_in, slab_own),
+                (grad_in, own),
                 (mask_res_in, mask_res),
                 (mask_slab_in, mask_slab),
                 (wbl, both_b.at[:, pl.ds(0, 128)]),
                 (wbg, both_b.at[:, pl.ds(128, 128)]),
                 (pair_in, pair_ref),
-                (grad_in, own),
-                (slab_in, slab_own),
                 (wal, both_a.at[:, pl.ds(0, 128)]),
                 (wag, both_a.at[:, pl.ds(128, 128)]),
             )
@@ -143,28 +143,9 @@
     ]
     for load in loads:
         load.start()
-    for load in loads:
+    pl.semaphore_wait(barrier, len(peers))
+    for load in loads[:2]:
         load.wait()
-    keys = key_mask(mask_res, me.row * 32)
-
-    def forward(n, first, mask, rows_ref, both, value, to_lin, to_gate):
-        rows = pl.ds(pl.multiple_of(n * 256, 256), 256)
-        flags = jnp.concatenate(
-            [keys * mask[first + n * 8 + m].astype(F32) for m in range(8)], axis=0
-        )
-        val, lin, gate = gates(rows_ref(n), both[...], flags)
-        value[rows, :] = val.astype(BF16).astype(F32)
-        to_lin[rows, :] = lin
-        to_gate[rows, :] = gate
-
-    @pl.loop(0, 8)
-    def _(n):
-        rows = pl.ds(pl.multiple_of(n * 256, 256), 256)
-        forward(n, me.col * 64, mask_res, lambda n: pair_ref[rows, :], both_b, pair_value, pair_lin, pair_gate)
-
-    sum_a[...] = jnp.zeros_like(sum_a)
-    sum_b[...] = jnp.zeros_like(sum_b)
-    pl.semaphore_wait(barrier, len(peers))
     out = Sender(send_sems, twin)
 
     def z_of(t):
@@ -186,6 +167,27 @@
         out.send(slab_own, slab_own, sx.at[0, d - 1], xs[d - 1])
     out.send(slab_own, slab_own, sc.at[0, 0], twin)
 
+    for load in loads[2:]:
+        load.wait()
+    keys = key_mask(mask_res, me.row * 32)
+
+    def forward(n, first, mask, rows_ref, both, value, to_lin, to_gate):
+        rows = pl.ds(pl.multiple_of(n * 256, 256), 256)
+        flags = jnp.concatenate(
+            [keys * mask[first + n * 8 + m].astype(F32) for m in range(8)], axis=0
+        )
+        val, lin, gate = gates(rows_ref(n), both[...], flags)
+        value[rows, :] = val.astype(BF16).astype(F32)
+        to_lin[rows, :] = lin
+        to_gate[rows, :] = gate
+
+    @pl.loop(0, 8)
+    def _(n):
+        rows = pl.ds(pl.multiple_of(n * 256, 256), 256)
+        forward(n, me.col * 64, mask_res, lambda n: pair_ref[rows, :], both_b, pair_value, pair_lin, pair_gate)
+
+    sum_a[...] = jnp.zeros_like(sum_a)
+    sum_b[...] = jnp.zeros_like(sum_b)
     def spread(t):
         out.recv(block(t), gz.at[t - 1])
         if t == 4:

time: 65.7 us -> 64.9 us (0.988)
  Pallas kernels: 65 us -> 64.2 us
    pallas_call x1, Pallas kernels: 64.1 us -> 63.3 us  [on_device(): pl.pallas_call(whole_kernel, out_shape=HELD, in_specs=[ANY] * 9, out_spec...]
where the time goes in v7:
time: 64.9 us; the launch traced here: 64.8 us
  Pallas kernels  64.2 us (99%)
    pallas_call x1, Pallas kernels, on_device(): pl.pallas_call(whole_kernel, out_shape=HELD, in_specs=[ANY] * 9, out_spec...  63.3 us

profile of v7, /device:TPU:1, one launch (start us, length us, event | category | flops | bytes accessed | tf_op | source)
XLA Modules:
  0.0 64.8 jit_solution(9911471332955156451)
XLA Ops:
  0.6 63.3 %whole.1 = (bf16[128,128]{1,0:T(8,128)(2,1)S(1)}, bf16[2048,128]{1,0:T(8,128)(2,1)S(1)}, f32[2,16,16,128]{3,2,1,0:T(8,128)S(1)}) custom-call(bf16[2,64,128]{2,1,0:T(8,128)(2,1)} %grad_in.1, bf16[4,32,128]{2,1,0:T(8,128)(2,1)} %slab_in.1, bf16[2048,128]{1,0:T(8,128)(2,1)} %bitcast.4, bf16[128,128]{1,0:T(8,128)(2,1)} %wal.1, bf16[128,128]{1,0:T(8,128)(2,1)} %wag.1, ...), custom_call_target="tpu_custom_call" | custom-call | tf_op jit(solution)/shard_map/whole/pallas_call | solution.py:462
  63.9 0.9 %settle.1 = (bf16[128,128]{1,0:T(8,128)(2,1)}, bf16[2048,128]{1,0:T(8,128)(2,1)}, f32[2,16,16,128]{3,2,1,0:T(8,128)}) custom-call(bf16[128,128]{1,0:T(8,128)(2,1)S(1)} %get-tuple-element.9.refs_0_, bf16[2048,128]{1,0:T(8,128)(2,1)S(1)} %get-tuple-element.10.refs_1_, f32[2,16,16,128]{3,2,1,0:T(8,128)S(1)} %get-tuple-element.11.refs_2_), custom_call_target="tpu_custom_call" | custom-call | tf_op jit(solution)/shard_map/settle/pallas_call | solution.py:447

commit v8 on v7

--- a/solution.py
+++ b/solution.py
@@ -193,6 +193,7 @@
         if t == 4:
             for d in (2, 1, 3):
                 out.send(block(t), block(t), gz.at[3 + d], group[d - 1])
+            out.send(slab_own, slab_own, sh.at[0], far)
         for d in (2, 1, 3):
             out.send(block(t), block(t), gy.at[t, d - 1], ys[d - 1])
 
@@ -309,9 +310,8 @@
     odd = (me.z + me.h) % 2
     for t in (1, 3, 2):
         spread(t)
+    spread(4)
     slab_round(0)
-    spread(4)
-    out.send(slab_own, slab_own, sh.at[0], far)
     slab_sum(0)
     slab_forward(0)
     slab_sum(1)

time: 64.9 us -> 64.8 us (level)
  no operation moved by 1% of the time
where the time goes in v8:
time: 64.8 us; the launch traced here: 64.7 us
  Pallas kernels  64.1 us (99%)
    pallas_call x1, Pallas kernels, on_device(): pl.pallas_call(whole_kernel, out_shape=HELD, in_specs=[ANY] * 9, out_spec...  63.2 us

profile of v8, /device:TPU:1, one launch (start us, length us, event | category | flops | bytes accessed | tf_op | source)
XLA Modules:
  0.0 64.7 jit_solution(2927528735397216643)
XLA Ops:
  0.6 63.2 %whole.1 = (bf16[128,128]{1,0:T(8,128)(2,1)S(1)}, bf16[2048,128]{1,0:T(8,128)(2,1)S(1)}, f32[2,16,16,128]{3,2,1,0:T(8,128)S(1)}) custom-call(bf16[2,64,128]{2,1,0:T(8,128)(2,1)} %grad_in.1, bf16[4,32,128]{2,1,0:T(8,128)(2,1)} %slab_in.1, bf16[2048,128]{1,0:T(8,128)(2,1)} %bitcast.4, bf16[128,128]{1,0:T(8,128)(2,1)} %wal.1, bf16[128,128]{1,0:T(8,128)(2,1)} %wag.1, ...), custom_call_target="tpu_custom_call" | custom-call | tf_op jit(solution)/shard_map/whole/pallas_call | solution.py:462
  63.8 0.9 %settle.1 = (bf16[128,128]{1,0:T(8,128)(2,1)}, bf16[2048,128]{1,0:T(8,128)(2,1)}, f32[2,16,16,128]{3,2,1,0:T(8,128)}) custom-call(bf16[128,128]{1,0:T(8,128)(2,1)S(1)} %get-tuple-element.9.refs_0_, bf16[2048,128]{1,0:T(8,128)(2,1)S(1)} %get-tuple-element.10.refs_1_, f32[2,16,16,128]{3,2,1,0:T(8,128)S(1)} %get-tuple-element.11.refs_2_), custom_call_target="tpu_custom_call" | custom-call | tf_op jit(solution)/shard_map/settle/pallas_call | solution.py:447
